TPU v7x, 768 devices: a whole 4x8x12 slice. The times are simulated.
768 devices in a mesh: strip: 8 (over y), wide: 48 (over z, x_hi, core), comp: 2 (over x_lo).
Axes of the slice: x: 4 (x_hi: 2, x_lo: 2; x = x_hi * 2 + x_lo), y: 8, z: 12, core: 2. Of those that a mesh axis runs over, the one named last changes fastest.
Arguments:
- spectrum: bfloat16 [1152, 98304], P('comp', ('strip', 'wide')), may hold values from 0.049804688 to 2
- wet_mask: int32 [384, 256], P('strip'), may hold values 0 or 1
- currents: float32 [2, 64, 192], P(None, 'strip', 'wide'), may hold values from -3 to 3
- remap_index: int32 [4, 98304], P(None, 'strip'), may hold values from 0 to 1535, as said below
- remap_weights: float32 [4, 98304], P(None, 'strip'), may hold values from 0.2 to 0.6
- source_matrix: bfloat16 [1152, 1152], P('comp'), may hold values from -0.1875 to 0.1875
Outputs:
- updated: bfloat16 [1152, 98304], P('comp', ('strip', 'wide'))
- stokes: float32 [2, 32, 98304], P(None, 'comp', ('strip', 'wide'))
Inputs may be any that keep to these rules, and one draw needn't show every extreme that they name: `remap_index`: a point's cells lie in the ocean rows and columns of its strip next to the point's own location.
All inputs are finite; a program needn't handle non-finite values. No bound on the sum of `wet_mask` on one device may be relied on, other than what follows from the above.
Results may differ from a plain program's by a relative error of at most 0.0048.
Values may be sent and summed in bfloat16 or wider, within the bound.
No kernel may reach another device: no remote copies, remote signals or barrier semaphores. Data moves between devices by JAX's collectives and lax.ppermute only.
A program may use at most 32 MiB of HBM per device.

v0:
```python
import math

import jax
import jax.numpy as jnp
from jax import lax
from jax.sharding import PartitionSpec as P

NFREQ = 32
NDIR = 36
LEVELS = 32
SUBSTEPS = 4


courant = 0.45


def extended(cells, sides, width):
    for axis, dim in sides:
        count = lax.axis_size(axis)
        ends = count - 1
        head = lax.slice_in_dim(cells, 0, width, axis=dim)
        tail = lax.slice_in_dim(cells, cells.shape[dim] - width, cells.shape[dim], axis=dim)
        cells = jnp.concatenate(
            [
                lax.ppermute(tail, axis, [(i, (i + 1) % count) for i in range(ends)]),
                cells,
                lax.ppermute(head, axis, [((i + 1) % count, i) for i in range(ends)]),
            ],
            axis=dim,
        )
    return cells


def bin_speeds(first_bin, bin_count):
    index = first_bin + jnp.arange(bin_count, dtype=jnp.int32)
    freq_index = (index // NDIR).astype(jnp.float32)
    dir_index = (index % NDIR).astype(jnp.float32)
    group_speed = 0.35 + 0.65 * (NFREQ - 1 - freq_index) / (NFREQ - 1)
    heading = 2.0 * math.pi * (dir_index + 0.5) / NDIR
    return (
        (group_speed * jnp.cos(heading))[:, None, None],
        (group_speed * jnp.sin(heading))[:, None, None],
    )


def stokes_kernel(bin_count, first_level, level_count):
    index = jnp.arange(bin_count, dtype=jnp.int32)
    frequency = (index // NDIR + 1).astype(jnp.float32)
    heading = 2.0 * math.pi * ((index % NDIR).astype(jnp.float32) + 0.5) / NDIR
    level_index = (first_level + jnp.arange(level_count, dtype=jnp.int32)).astype(jnp.float32)
    damping = jnp.exp(-4.0 * frequency[None, :] * (level_index[:, None] + 0.5) / (NFREQ * LEVELS))
    amplitude = damping * (frequency / NFREQ)[None, :] / math.sqrt(NDIR)
    eastward = amplitude * jnp.cos(heading)[None, :]
    northward = amplitude * jnp.sin(heading)[None, :]
    return jnp.concatenate([eastward, northward], 0).astype(jnp.bfloat16)


def substep(energy, east_flow, north_flow, wet_frac, speed_east, speed_north):
    east_speed = speed_east + east_flow[None]
    north_speed = speed_north + north_flow[None]
    flux_lon = jnp.maximum(east_speed, 0.0) * energy + jnp.minimum(
        jnp.roll(east_speed, -1, 2), 0.0
    ) * jnp.roll(energy, -1, 2)
    flux_lat = (
        jnp.maximum(north_speed[:, :-1], 0.0) * energy[:, :-1]
        + jnp.minimum(north_speed[:, 1:], 0.0) * energy[:, 1:]
    )
    spread = flux_lon - jnp.roll(flux_lon, 1, 2)
    change = spread[:, 1:-1] + flux_lat[:, 1:] - flux_lat[:, :-1]
    return wet_frac[1:-1] * (energy[:, 1:-1] - courant * change)


def advance(widened, speed_east, speed_north):
    bin_share = speed_east.shape[0]
    energy = widened[:bin_share]
    east_flow = widened[bin_share]
    north_flow = widened[bin_share + 1]
    wet_frac = widened[bin_share + 2]
    energy = substep(energy, east_flow, north_flow, wet_frac, speed_east, speed_north)
    return energy


def extend(fields, margin):
    return extended(fields, (("strip", 1),), margin)


def interpolate(tiles, remap_index, remap_weights, lat_rows, lon_cells):
    ocean_rows = tiles.shape[1]
    ocean_cols = tiles.shape[2]
    block_points = 4 * lon_cells
    block_count = lat_rows // 4
    flow_table = tiles.reshape(2 * ocean_rows, ocean_cols)
    index_blocks = jnp.transpose(remap_index.reshape(4, block_count, block_points), (1, 0, 2))
    weight_blocks = jnp.transpose(remap_weights.reshape(4, block_count, block_points), (1, 0, 2))
    column_ids = jnp.arange(ocean_cols, dtype=jnp.int32)[None, :, None]
    row_ids = jnp.arange(ocean_rows, dtype=jnp.int32)[None, :, None]

    def one_block(inputs):
        cells, shares = inputs
        column_of = cells % ocean_cols
        row_of = cells // ocean_cols
        column_hot = (column_of[:, None, :] == column_ids).astype(jnp.float32)
        picked = jnp.einsum("mk,jkp->jmp", flow_table, column_hot, precision=lax.Precision.HIGHEST)
        picked = picked.reshape(4, 2, ocean_rows, block_points)
        row_weight = (row_of[:, None, :] == row_ids).astype(jnp.float32) * shares[:, None, :]
        return jnp.sum(picked * row_weight[:, None], (0, 2))

    blocks = lax.map(one_block, (index_blocks, weight_blocks))
    return jnp.transpose(blocks, (1, 0, 2)).reshape(2, lat_rows, lon_cells)


def per_device(spectrum, wet_mask, currents, remap_index, remap_weights, source_matrix):
    wide_index = lax.axis_index("wide")
    comp_index = lax.axis_index("comp")
    lat_rows, lon_cells = wet_mask.shape
    local_bins, points = spectrum.shape
    tiles = lax.all_gather(currents, "wide", axis=2, tiled=True)
    surface = interpolate(tiles, remap_index, remap_weights, lat_rows, lon_cells)
    wet_frac = wet_mask.astype(jnp.float32)
    arrived = lax.all_to_all(spectrum, "wide", split_axis=0, concat_axis=1, tiled=True)
    bin_share = arrived.shape[0]
    first_bin = comp_index * local_bins + wide_index * bin_share
    speed_east, speed_north = bin_speeds(first_bin, bin_share)
    energy = arrived.astype(jnp.float32).reshape(bin_share, lat_rows, lon_cells) * wet_frac
    for repeat in range(SUBSTEPS):
        fields = jnp.concatenate([energy, surface, wet_frac[None]], 0)
        energy = advance(extend(fields, 1), speed_east, speed_north)
    propagated = energy.astype(jnp.bfloat16).reshape(bin_share, lat_rows * lon_cells)
    returned = lax.all_to_all(propagated, "wide", split_axis=1, concat_axis=0, tiled=True)
    level_rows = LEVELS // lax.axis_size("comp")
    first_level = comp_index * level_rows
    fragment = lax.all_gather(returned, "comp", axis=0, tiled=True)
    width = fragment.shape[0]
    kernel = stokes_kernel(width, first_level, level_rows)
    source_part = jnp.dot(source_matrix, fragment, preferred_element_type=jnp.float32)
    drift_part = jnp.dot(kernel, fragment, preferred_element_type=jnp.float32)
    wet_points = lax.dynamic_slice_in_dim(wet_frac.reshape(-1), wide_index * points, points, 0)
    updated = (
        wet_points[None, :] * jnp.maximum(returned.astype(jnp.float32) + source_part, 0.0)
    ).astype(jnp.bfloat16)
    return (updated, drift_part.reshape(2, level_rows, points))


def solution(mesh):
    placed = (
        P("comp", ("strip", "wide")),
        P("strip", None),
        P(None, "strip", "wide"),
        P(None, "strip"),
        P(None, "strip"),
        P("comp", None),
    )
    return jax.shard_map(
        per_device,
        mesh=mesh,
        in_specs=placed,
        out_specs=(P("comp", ("strip", "wide")), P(None, "comp", ("strip", "wide"))),
        check_vma=False,
    )
```

profile of v0, /device:TPU:1, one launch (start us, length us, event | category | flops | bytes accessed | tf_op | source)
XLA Modules:
  0.0 214.0 jit_solution(12623357811934981793)
XLA Ops:
  0.7 1.9 all_to_all.22
  2.5 19.4 %all-to-all-start = ((bf16[48,12,256]{2,1,0:T(8,128)(2,1)}), bf16[48,12,256]{2,1,0:T(8,128)(2,1)S(1)}, u32[]{:S(2)}, u32[]{:S(2)}) async-start(bf16[48,12,256]{2,1,0:T(8,128)(2,1)} %all_to_all.22), calls=%async_computation | async-start | bytes 786432 | tf_op jit(solution)/shard_map/all_to_all | solution.py:120
  22.0 65.0 %all_gather.6 = f32[2,8,192]{1,0,2:T(2,128)S(1)} all-gather(f32[2,8,4]{1,0,2:T(2,128)S(1)} %copy.18), channel_id=1, replica_groups=mesh['strip'=8,'wide'=48,'comp'=2] {'wide'}, dimensions={2}, use_global_device_ids=true | all-gather | bytes 12544 | tf_op jit(solution)/shard_map/all_gather | solution.py:117
  87.1 31.8 %while.13 = (s32[]{:T(128)}, f32[12,2,1024]{2,1,0:T(2,128)S(1)}, s32[12,4,1024]{2,1,0:T(4,128)}, f32[16,192]{1,0:T(8,128)S(1)}, f32[12,4,1024]{2,1,0:T(4,128)}, /*index=5*/s32[]{:T(128)}) while((s32[]{:T(128)}, f32[12,2,1024]{2,1,0:T(2,128)S(1)}, s32[12,4,1024]{2,1,0:T(4,128)}, f32[16,192]{1,0:T(8,128)S(1)}, ...), condition=%wide.region_3.4_spmd.clone, body=%wide.region_0.3_spmd.clone.sunk | while | flops 152025088 | bytes 561233 | solution.py:108
  87.1 0.8 add_select_fusion.4
  87.8 0.7 dynamic-slice_bitcast_fusion.2
  88.6 1.1 fusion.108
  89.7 0.8 add_select_fusion.4
  91.2 1.1 fusion.108
  92.4 0.8 add_select_fusion.4
  93.9 1.1 fusion.108
  95.0 0.8 add_select_fusion.4
  95.8 0.7 dynamic-slice_bitcast_fusion.2
  96.5 1.1 fusion.108
  97.7 0.8 add_select_fusion.4
  99.2 1.1 fusion.108
  100.3 0.8 add_select_fusion.4
  101.8 1.1 fusion.108
  103.0 0.8 add_select_fusion.4
  104.5 1.1 fusion.108
  105.6 0.8 add_select_fusion.4
  107.1 1.1 fusion.108
  108.2 0.8 add_select_fusion.4
  109.8 1.1 fusion.108
  110.9 0.8 add_select_fusion.4
  112.4 1.1 fusion.108
  113.5 0.8 add_select_fusion.4
  115.0 1.1 fusion.108
  116.2 0.8 add_select_fusion.4
  117.7 1.1 fusion.108
  119.2 3.2 %collective-permute-start = (f32[15,1,256]{2,0,1:T(8,128)S(1)}, f32[15,1,256]{2,0,1:T(8,128)S(1)}, u32[]{:S(2)}, u32[]{:S(2)}) collective-permute-start(f32[15,1,256]{2,0,1:T(8,128)S(1)} %get-tuple-element.139), channel_id=1, source_target_pairs={{0,96},{96,192},{192,288},{288,384},{384,480},{480,576},{576,672},... | collective-permute-start | bytes 46088 | tf_op jit(solution)/shard_map/ppermute | solution.py:25
  122.4 1.3 collective-permute-start.1
  123.8 3.1 %collective-permute-done.1 = f32[15,1,256]{2,0,1:T(8,128)S(1)} collective-permute-done((f32[15,1,256]{2,0,1:T(8,128)S(1)}, f32[15,1,256]{2,0,1:T(8,128)S(1)}, u32[]{:S(2)}, u32[]{:S(2)}) %collective-permute-start.1) | collective-permute-done | bytes 15392 | tf_op jit(solution)/shard_map/ppermute | solution.py:27
  129.7 3.2 %collective-permute-start.2 = (f32[15,1,256]{2,0,1:T(8,128)S(1)}, f32[15,1,256]{2,0,1:T(8,128)S(1)}, u32[]{:S(2)}, u32[]{:S(2)}) collective-permute-start(f32[15,1,256]{2,0,1:T(8,128)S(1)} %get-tuple-element.137), channel_id=1, source_target_pairs={{0,96},{96,192},{192,288},{288,384},{384,480},{480,576},{576,672},... | collective-permute-start | bytes 46088 | tf_op jit(solution)/shard_map/ppermute | solution.py:25
  132.9 1.3 collective-permute-start.3
  134.2 4.1 %collective-permute-done.3 = f32[15,1,256]{2,0,1:T(8,128)S(1)} collective-permute-done((f32[15,1,256]{2,0,1:T(8,128)S(1)}, f32[15,1,256]{2,0,1:T(8,128)S(1)}, u32[]{:S(2)}, u32[]{:S(2)}) %collective-permute-start.3) | collective-permute-done | bytes 15392 | tf_op jit(solution)/shard_map/ppermute | solution.py:27
  141.1 4.6 %collective-permute-start.4 = (f32[15,1,256]{2,0,1:T(8,128)S(1)}, f32[15,1,256]{2,0,1:T(8,128)S(1)}, u32[]{:S(2)}, u32[]{:S(2)}) collective-permute-start(f32[15,1,256]{2,0,1:T(8,128)S(1)} %get-tuple-element.135), channel_id=1, source_target_pairs={{0,96},{96,192},{192,288},{288,384},{384,480},{480,576},{576,672},... | collective-permute-start | bytes 46088 | tf_op jit(solution)/shard_map/ppermute | solution.py:25
  145.7 1.3 collective-permute-start.5
  147.0 3.2 %collective-permute-done.5 = f32[15,1,256]{2,0,1:T(8,128)S(1)} collective-permute-done((f32[15,1,256]{2,0,1:T(8,128)S(1)}, f32[15,1,256]{2,0,1:T(8,128)S(1)}, u32[]{:S(2)}, u32[]{:S(2)}) %collective-permute-start.5) | collective-permute-done | bytes 15392 | tf_op jit(solution)/shard_map/ppermute | solution.py:27
  153.0 3.5 %collective-permute-start.6 = (f32[15,1,256]{2,0,1:T(8,128)S(1)}, f32[15,1,256]{2,0,1:T(8,128)S(1)}, u32[]{:S(2)}, u32[]{:S(2)}) collective-permute-start(f32[15,1,256]{2,0,1:T(8,128)S(1)} %get-tuple-element.133), channel_id=1, source_target_pairs={{0,96},{96,192},{192,288},{288,384},{384,480},{480,576},{576,672},... | collective-permute-start | bytes 46088 | tf_op jit(solution)/shard_map/ppermute | solution.py:25
  156.5 1.5 collective-permute-start.7
  158.0 3.0 %collective-permute-done.7 = f32[15,1,256]{2,0,1:T(8,128)S(1)} collective-permute-done((f32[15,1,256]{2,0,1:T(8,128)S(1)}, f32[15,1,256]{2,0,1:T(8,128)S(1)}, u32[]{:S(2)}, u32[]{:S(2)}) %collective-permute-start.7) | collective-permute-done | bytes 15392 | tf_op jit(solution)/shard_map/ppermute | solution.py:27
  163.2 1.2 fusion.57
  164.4 15.7 %all-to-all-start.1 = ((bf16[12,48,256]{2,0,1:T(8,128)(2,1)}), bf16[12,48,256]{2,0,1:T(8,128)(2,1)S(1)}, u32[]{:S(2)}, u32[]{:S(2)}) async-start(bf16[12,48,256]{2,0,1:T(8,128)(2,1)} %fusion.57), calls=%async_computation.1 | async-start | bytes 786432 | tf_op jit(solution)/shard_map/all_to_all | solution.py:129
  180.4 22.4 %all-to-all-done.1 = bf16[12,48,256]{2,0,1:T(8,128)(2,1)S(1)} async-done(((bf16[12,48,256]{2,0,1:T(8,128)(2,1)}), bf16[12,48,256]{2,0,1:T(8,128)(2,1)S(1)}, u32[]{:S(2)}, u32[]{:S(2)}) %all-to-all-start.1) | async-done | bytes 294944 | tf_op jit(solution)/shard_map/all_to_all | solution.py:129
  202.9 9.0 %all_gather.7 = bf16[1152,256]{1,0:T(8,128)(2,1)S(1)} all-gather(bf16[576,256]{1,0:T(8,128)(2,1)S(1)} %all_to_all.26), channel_id=1, replica_groups=mesh['strip'=8,'wide'=48,'comp'=2] {'comp'}, dimensions={0}, use_global_device_ids=true | all-gather | bytes 884736 | tf_op jit(solution)/shard_map/all_gather | solution.py:132
  211.9 1.3 fusion.17
  213.2 0.8 fusion.67
  (133 shorter events, 19.2 us)
Async XLA Ops:
  0.6 211.3 %copy-start = (bf16[576,1152]{1,0:T(8,128)(2,1)S(1)}, bf16[576,1152]{1,0:T(8,128)(2,1)}, u32[]{:S(2)}) copy-start(bf16[576,1152]{1,0:T(8,128)(2,1)} %param.13) | copy-start | bytes 3981316
  0.6 21.3 %copy-start.2 = (f32[2,8,4]{1,2,0:T(4,128)S(1)}, f32[2,8,4]{1,2,0:T(4,128)}, u32[]{:S(2)}) copy-start(f32[2,8,4]{1,2,0:T(4,128)} %param.10) | copy-start | bytes 772
  2.5 116.4 %all-to-all-start = ((bf16[48,12,256]{2,1,0:T(8,128)(2,1)}), bf16[48,12,256]{2,1,0:T(8,128)(2,1)S(1)}, u32[]{:S(2)}, u32[]{:S(2)}) async-start(bf16[48,12,256]{2,1,0:T(8,128)(2,1)} %all_to_all.22), calls=%async_computation | async-start | bytes 786432 | tf_op jit(solution)/shard_map/all_to_all | solution.py:120
  87.1 31.8 %copy-start.1 = (s32[48,256]{1,0:T(8,128)S(1)}, s32[48,256]{1,0:T(8,128)}, u32[]{:S(2)}) copy-start(s32[48,256]{1,0:T(8,128)} %param.9) | copy-start | bytes 147460
  119.2 4.6 %collective-permute-start = (f32[15,1,256]{2,0,1:T(8,128)S(1)}, f32[15,1,256]{2,0,1:T(8,128)S(1)}, u32[]{:S(2)}, u32[]{:S(2)}) collective-permute-start(f32[15,1,256]{2,0,1:T(8,128)S(1)} %get-tuple-element.139), channel_id=1, source_target_pairs={{0,96},{96,192},{192,288},{288,384},{384,480},{480,576},{576,672},... | collective-permute-start | bytes 46088 | tf_op jit(solution)/shard_map/ppermute | solution.py:25
  122.4 4.5 %collective-permute-start.1 = (f32[15,1,256]{2,0,1:T(8,128)S(1)}, f32[15,1,256]{2,0,1:T(8,128)S(1)}, u32[]{:S(2)}, u32[]{:S(2)}) collective-permute-start(f32[15,1,256]{2,0,1:T(8,128)S(1)} %get-tuple-element.140), channel_id=1, source_target_pairs={{96,0},{192,96},{288,192},{384,288},{480,384},{576,480},{672,576},... | collective-permute-start | bytes 46088 | tf_op jit(solution)/shard_map/ppermute | solution.py:27
  129.7 4.5 %collective-permute-start.2 = (f32[15,1,256]{2,0,1:T(8,128)S(1)}, f32[15,1,256]{2,0,1:T(8,128)S(1)}, u32[]{:S(2)}, u32[]{:S(2)}) collective-permute-start(f32[15,1,256]{2,0,1:T(8,128)S(1)} %get-tuple-element.137), channel_id=1, source_target_pairs={{0,96},{96,192},{192,288},{288,384},{384,480},{480,576},{576,672},... | collective-permute-start | bytes 46088 | tf_op jit(solution)/shard_map/ppermute | solution.py:25
  132.9 5.4 %collective-permute-start.3 = (f32[15,1,256]{2,0,1:T(8,128)S(1)}, f32[15,1,256]{2,0,1:T(8,128)S(1)}, u32[]{:S(2)}, u32[]{:S(2)}) collective-permute-start(f32[15,1,256]{2,0,1:T(8,128)S(1)} %get-tuple-element.138), channel_id=1, source_target_pairs={{96,0},{192,96},{288,192},{384,288},{480,384},{576,480},{672,576},... | collective-permute-start | bytes 46088 | tf_op jit(solution)/shard_map/ppermute | solution.py:27
  141.1 5.9 %collective-permute-start.4 = (f32[15,1,256]{2,0,1:T(8,128)S(1)}, f32[15,1,256]{2,0,1:T(8,128)S(1)}, u32[]{:S(2)}, u32[]{:S(2)}) collective-permute-start(f32[15,1,256]{2,0,1:T(8,128)S(1)} %get-tuple-element.135), channel_id=1, source_target_pairs={{0,96},{96,192},{192,288},{288,384},{384,480},{480,576},{576,672},... | collective-permute-start | bytes 46088 | tf_op jit(solution)/shard_map/ppermute | solution.py:25
  145.7 4.5 %collective-permute-start.5 = (f32[15,1,256]{2,0,1:T(8,128)S(1)}, f32[15,1,256]{2,0,1:T(8,128)S(1)}, u32[]{:S(2)}, u32[]{:S(2)}) collective-permute-start(f32[15,1,256]{2,0,1:T(8,128)S(1)} %get-tuple-element.136), channel_id=1, source_target_pairs={{96,0},{192,96},{288,192},{384,288},{480,384},{576,480},{672,576},... | collective-permute-start | bytes 46088 | tf_op jit(solution)/shard_map/ppermute | solution.py:27
  153.0 5.0 %collective-permute-start.6 = (f32[15,1,256]{2,0,1:T(8,128)S(1)}, f32[15,1,256]{2,0,1:T(8,128)S(1)}, u32[]{:S(2)}, u32[]{:S(2)}) collective-permute-start(f32[15,1,256]{2,0,1:T(8,128)S(1)} %get-tuple-element.133), channel_id=1, source_target_pairs={{0,96},{96,192},{192,288},{288,384},{384,480},{480,576},{576,672},... | collective-permute-start | bytes 46088 | tf_op jit(solution)/shard_map/ppermute | solution.py:25
  156.5 4.5 %collective-permute-start.7 = (f32[15,1,256]{2,0,1:T(8,128)S(1)}, f32[15,1,256]{2,0,1:T(8,128)S(1)}, u32[]{:S(2)}, u32[]{:S(2)}) collective-permute-start(f32[15,1,256]{2,0,1:T(8,128)S(1)} %get-tuple-element.134), channel_id=1, source_target_pairs={{96,0},{192,96},{288,192},{384,288},{480,384},{576,480},{672,576},... | collective-permute-start | bytes 46088 | tf_op jit(solution)/shard_map/ppermute | solution.py:27
  164.4 38.4 %all-to-all-start.1 = ((bf16[12,48,256]{2,0,1:T(8,128)(2,1)}), bf16[12,48,256]{2,0,1:T(8,128)(2,1)S(1)}, u32[]{:S(2)}, u32[]{:S(2)}) async-start(bf16[12,48,256]{2,0,1:T(8,128)(2,1)} %fusion.57), calls=%async_computation.1 | async-start | bytes 786432 | tf_op jit(solution)/shard_map/all_to_all | solution.py:129
where the time goes:
time: 217 us; the launch traced here: 214 us
  blocking collectives  74 us (34%)
  starting transfers between devices  54.9 us (25%)
  waiting for transfers between devices  35.7 us (16%)
  other arithmetic  18.2 us (8%)
  matrix products  15 us (7%)
  local copies, waits for them, and re-layouts  14.6 us (7%)
    all_gather x1, blocking collectives, per_device(): tiles = lax.all_gather(currents, 'wide', axis=2, tiled=True)  65 us
    all_to_all x1, waiting for transfers between devices, per_device(): lax.all_to_all(propagated, 'wide', split_axis=1, concat_axis=0, tiled=True)  22.4 us
    all_to_all x1, starting transfers between devices, per_device(): lax.all_to_all(spectrum, 'wide', split_axis=0, concat_axis=1, tiled=True)  19.4 us
    all_to_all x1, starting transfers between devices, per_device(): lax.all_to_all(propagated, 'wide', split_axis=1, concat_axis=0, tiled=True)  15.7 us
    ppermute x4, starting transfers between devices, extended(): lax.ppermute(tail, axis, [(i, (i + 1) % count) for i in range(ends)])  14.5 us
    ppermute x4, waiting for transfers between devices, extended(): lax.ppermute(head, axis, [((i + 1) % count, i) for i in range(ends)])  13.4 us
    dot_general x12, matrix products, one_block(): jnp.einsum('mk,jkp->jmp', flow_table, column_hot, precision=lax.Precision...  12.9 us
    select_n x12, other arithmetic, one_block(): row_of = cells // ocean_cols  9.08 us
  transfers between devices with their start and end apart: 10, of which 5 were waited for; matrix products, arithmetic and copies ran while one was open for 15% of the time, Pallas kernels for 0%

commit v1 on v0

v1 whole, which is shorter than its diff:
```python
import math

import jax
import jax.numpy as jnp
from jax import lax
from jax.experimental import pallas as pl
from jax.experimental.pallas import tpu as pltpu
from jax.sharding import PartitionSpec as P

NFREQ = 32
NDIR = 36
LEVELS = 32
SUBSTEPS = 4
OCEAN_ROWS = 8
OCEAN_COLS = 192
ROWS = 4

courant = 0.45


def bin_speeds(first_bin, bin_count):
    index = first_bin + jnp.arange(bin_count, dtype=jnp.int32)
    freq_index = (index // NDIR).astype(jnp.float32)
    dir_index = (index % NDIR).astype(jnp.float32)
    group_speed = 0.35 + 0.65 * (NFREQ - 1 - freq_index) / (NFREQ - 1)
    heading = 2.0 * math.pi * (dir_index + 0.5) / NDIR
    speed_east = courant * group_speed * jnp.cos(heading)
    speed_north = courant * group_speed * jnp.sin(heading)
    return (
        jnp.broadcast_to(speed_east[:, None], (bin_count, 128)),
        jnp.broadcast_to(speed_north[:, None], (bin_count, 128)),
    )


def stokes_kernel(bin_count, first_level, level_count):
    index = jnp.arange(bin_count, dtype=jnp.int32)
    frequency = (index // NDIR + 1).astype(jnp.float32)
    heading = 2.0 * math.pi * ((index % NDIR).astype(jnp.float32) + 0.5) / NDIR
    level_index = (first_level + jnp.arange(level_count, dtype=jnp.int32)).astype(jnp.float32)
    damping = jnp.exp(-4.0 * frequency[None, :] * (level_index[:, None] + 0.5) / (NFREQ * LEVELS))
    amplitude = damping * (frequency / NFREQ)[None, :] / math.sqrt(NDIR)
    eastward = amplitude * jnp.cos(heading)[None, :]
    northward = amplitude * jnp.sin(heading)[None, :]
    return jnp.concatenate([eastward, northward], 0).astype(jnp.bfloat16)


def interpolate_body(table_ref, index_ref, weight_ref, mask_ref, out_ref):
    rows, cols = mask_ref.shape
    row_ids = lax.broadcasted_iota(jnp.int32, (OCEAN_ROWS, 128), 0)
    tables = [table_ref[q] for q in range(4)]
    for chunk in range(rows * cols // 128):
        lanes = slice(chunk * 128, chunk * 128 + 128)
        cells = index_ref[:, lanes]
        shares = weight_ref[:, lanes]
        row_of = (cells * 5462) >> 20
        column_of = cells - row_of * OCEAN_COLS
        lane_of = (column_of >> 4) * 8 + (column_of & 3)
        quarter_of = (column_of >> 2) & 3
        totals = [jnp.zeros((OCEAN_ROWS, 128), jnp.float32) for _ in range(2)]
        for corner in range(4):
            row_b = jnp.broadcast_to(row_of[corner : corner + 1], (OCEAN_ROWS, 128))
            lane_b = jnp.broadcast_to(lane_of[corner : corner + 1], (OCEAN_ROWS, 128))
            quarter_b = jnp.broadcast_to(quarter_of[corner : corner + 1], (OCEAN_ROWS, 128))
            share_b = jnp.broadcast_to(shares[corner : corner + 1], (OCEAN_ROWS, 128))
            weight = jnp.where(row_b == row_ids, share_b, 0.0)
            for c in range(2):
                picked = jnp.take_along_axis(tables[0], lane_b + 4 * c, axis=1)
                for q in range(1, 4):
                    other = jnp.take_along_axis(tables[q], lane_b + 4 * c, axis=1)
                    picked = jnp.where(quarter_b == q, other, picked)
                totals[c] += picked * weight
        row = chunk * 128 // cols
        spot = slice(chunk * 128 % cols, chunk * 128 % cols + 128)
        for c in range(2):
            out_ref[c * rows + row : c * rows + row + 1, spot] = courant * jnp.sum(
                totals[c], axis=0, keepdims=True
            )
    out_ref[2 * rows : 3 * rows, :] = mask_ref[...].astype(jnp.float32)
    out_ref[3 * rows :, :] = jnp.zeros((rows, cols), jnp.float32)


def interpolate(table, cells, shares, mask):
    rows, cols = mask.shape
    return pl.pallas_call(
        interpolate_body,
        out_shape=jax.ShapeDtypeStruct((4 * rows, cols), jnp.float32),
        in_specs=[pl.BlockSpec(memory_space=pltpu.VMEM)] * 4,
        out_specs=pl.BlockSpec(memory_space=pltpu.VMEM),
        cost_estimate=pl.CostEstimate(flops=2_000_000, bytes_accessed=100_000, transcendentals=0),
        name="interpolate",
    )(table, cells, shares, mask)


def propagate_body(
    below_ref, own_ref, above_ref, fbelow_ref, fown_ref, fabove_ref, east_ref, north_ref, out_ref
):
    rows, bins, cols = own_ref.shape
    tile = 16

    def one_tile(t, carry):
        spot = pl.ds(pl.multiple_of(t * tile, tile), tile)
        speed_east = jnp.concatenate([east_ref[spot, :]] * (cols // 128), 1)
        speed_north = jnp.concatenate([north_ref[spot, :]] * (cols // 128), 1)
        energy, masks = [], []
        coefs = []
        for source, fields in ((below_ref, fbelow_ref), (own_ref, fown_ref), (above_ref, fabove_ref)):
            for row in range(rows):
                mask = fields[2 * rows + row : 2 * rows + row + 1, :]
                east = speed_east + fields[row : row + 1, :]
                north = speed_north + fields[rows + row : rows + row + 1, :]
                to_east = jnp.maximum(east, 0.0)
                to_north = jnp.maximum(north, 0.0)
                stay = (1.0 - jnp.abs(east)) - jnp.abs(north)
                coefs.append((stay, to_east, to_east - east, to_north, to_north - north))
                energy.append(source[row, spot, :].astype(jnp.float32) * mask)
                masks.append(mask)
        count = 3 * rows
        for step in range(SUBSTEPS):
            low, high = step + 1, count - 1 - step
            fresh = list(energy)
            for i in range(low, high):
                stay, to_east, to_west, _, _ = coefs[i]
                moved = stay * energy[i]
                moved += pltpu.roll(to_east * energy[i], 1, 1)
                moved += pltpu.roll(to_west * energy[i], cols - 1, 1)
                moved += coefs[i - 1][3] * energy[i - 1]
                moved += coefs[i + 1][4] * energy[i + 1]
                fresh[i] = moved * masks[i]
            energy = fresh
        for row in range(rows):
            result = energy[rows + row].astype(jnp.bfloat16)
            out_ref[row, spot, :] = result
            out_ref[rows + row, spot, :] = result
        return carry

    lax.fori_loop(0, bins // tile, one_tile, 0)


def propagate(below, own, above, fbelow, fown, fabove, east, north):
    rows, bins, cols = own.shape
    return pl.pallas_call(
        propagate_body,
        out_shape=jax.ShapeDtypeStruct((2 * rows, bins, cols), jnp.bfloat16),
        in_specs=[pl.BlockSpec(memory_space=pltpu.VMEM)] * 8,
        out_specs=pl.BlockSpec(memory_space=pltpu.VMEM),
        cost_estimate=pl.CostEstimate(flops=40_000_000, bytes_accessed=1_600_000, transcendentals=0),
        name="propagate",
    )(below, own, above, fbelow, fown, fabove, east, north)


def per_device(spectrum, wet_mask, currents, remap_index, remap_weights, source_matrix):
    wide_index = lax.axis_index("wide")
    comp_index = lax.axis_index("comp")
    strips, wides = lax.axis_size("strip"), lax.axis_size("wide")
    comps = lax.axis_size("comp")
    lat_rows, lon_cells = wet_mask.shape
    local_bins, points = spectrum.shape
    groups = wides // ROWS
    group_index = wide_index // ROWS
    member = wide_index % ROWS
    share = local_bins // ROWS
    near = [[ROWS * g + i for i in range(ROWS)] for g in range(groups)]
    far = [[ROWS * g + i for g in range(groups)] for i in range(ROWS)]

    lane = jnp.arange(128, dtype=jnp.int32)
    ours = jnp.concatenate([currents[0], currents[1]], axis=1)
    ours = jnp.where((lane // 8 == group_index)[None, :], jnp.tile(ours, (1, 16)), 0.0)
    along = lax.all_to_all(
        jnp.broadcast_to(ours[None], (groups, OCEAN_ROWS, 128)),
        "wide", split_axis=0, concat_axis=0, tiled=True, axis_index_groups=far,
    )
    along = jnp.sum(along, 0)
    table = lax.all_to_all(
        jnp.broadcast_to(along[None], (ROWS, OCEAN_ROWS, 128)),
        "wide", split_axis=0, concat_axis=0, tiled=True, axis_index_groups=near,
    )

    own = lax.all_to_all(
        spectrum.reshape(ROWS, share, points),
        "wide", split_axis=0, concat_axis=0, tiled=True, axis_index_groups=near,
    )
    total = strips * wides
    upward = [(i, i + ROWS) for i in range(total - ROWS)]
    downward = [(i + ROWS, i) for i in range(total - ROWS)]
    chain = ("strip", "wide")
    below = lax.ppermute(own, chain, upward)
    above = lax.ppermute(own, chain, downward)

    first = group_index * ROWS * lon_cells
    cells = lax.dynamic_slice_in_dim(remap_index, first, ROWS * lon_cells, 1)
    shares = lax.dynamic_slice_in_dim(remap_weights, first, ROWS * lon_cells, 1)
    mask = lax.dynamic_slice_in_dim(wet_mask, group_index * ROWS, ROWS, 0)
    fown = interpolate(table, cells, shares, mask)
    fbelow = lax.ppermute(fown, chain, upward)
    fabove = lax.ppermute(fown, chain, downward)

    first_bin = comp_index * local_bins + member * share
    east, north = bin_speeds(first_bin, share)
    spread = propagate(below, own, above, fbelow, fown, fabove, east, north)

    both = [
        [(ROWS * g + i) * comps + k for k in range(comps) for i in range(ROWS)] for g in range(groups)
    ]
    fragment = lax.all_to_all(
        spread, ("wide", "comp"), split_axis=0, concat_axis=0, tiled=True, axis_index_groups=both
    ).reshape(comps * local_bins, points)

    level_rows = LEVELS // comps
    kernel = stokes_kernel(comps * local_bins, comp_index * level_rows, level_rows)
    source_part = jnp.dot(source_matrix, fragment, preferred_element_type=jnp.float32)
    drift_part = jnp.dot(kernel, fragment, preferred_element_type=jnp.float32)
    returned = lax.dynamic_slice_in_dim(fragment, comp_index * local_bins, local_bins, 0)
    wet_points = lax.dynamic_slice_in_dim(wet_mask, wide_index, 1, 0).astype(jnp.float32)
    updated = (
        wet_points * jnp.maximum(returned.astype(jnp.float32) + source_part, 0.0)
    ).astype(jnp.bfloat16)
    return (updated, drift_part.reshape(2, level_rows, points))


def solution(mesh):
    placed = (
        P("comp", ("strip", "wide")),
        P("strip", None),
        P(None, "strip", "wide"),
        P(None, "strip"),
        P(None, "strip"),
        P("comp", None),
    )
    return jax.shard_map(
        per_device,
        mesh=mesh,
        in_specs=placed,
        out_specs=(P("comp", ("strip", "wide")), P(None, "comp", ("strip", "wide"))),
        check_vma=False,
    )
```

time: 217 us -> 86.7 us (0.40)
  the two profiles are of different devices: /device:TPU:1 before, /device:TPU:32 now
where the time goes in v1:
time: 86.7 us; the launch traced here: 85.8 us
  starting transfers between devices  44.7 us (52%)
  waiting for transfers between devices  21.3 us (25%)
  local copies, waits for them, and re-layouts  8.23 us (9%)
  Pallas kernels  7.68 us (9%)
  matrix products  2.11 us (2%)
  other arithmetic  0.98 us (1%)
    all_to_all x1, starting transfers between devices, per_device(): lax.all_to_all(jnp.broadcast_to(ours[None], (groups, OCEAN_ROWS, 128)), '...  15.2 us
    all_to_all x1, waiting for transfers between devices, per_device(): lax.all_to_all(spread, ('wide', 'comp'), split_axis=0, concat_axis=0, til...  10.6 us
    ppermute x1, starting transfers between devices, per_device(): fabove = lax.ppermute(fown, chain, downward)  6.6 us
    pallas_call x1, Pallas kernels, propagate(): pl.pallas_call(propagate_body, out_shape=jax.ShapeDtypeStruct((2 * rows,...  5.77 us
    ppermute x1, starting transfers between devices, per_device(): above = lax.ppermute(own, chain, downward)  5.27 us
    all_to_all x1, waiting for transfers between devices, per_device(): lax.all_to_all(jnp.broadcast_to(along[None], (ROWS, OCEAN_ROWS, 128)), 'w...  4.62 us
    all_to_all x1, starting transfers between devices, per_device(): lax.all_to_all(spectrum.reshape(ROWS, share, points), 'wide', split_axis=...  4.44 us
    all_to_all x1, waiting for transfers between devices, per_device(): lax.all_to_all(spectrum.reshape(ROWS, share, points), 'wide', split_axis=...  4.21 us
  transfers between devices with their start and end apart: 8, of which 5 were waited for; matrix products, arithmetic and copies ran while one was open for 7% of the time, Pallas kernels for 2%

profile of v1, /device:TPU:32, one launch (start us, length us, event | category | flops | bytes accessed | tf_op | source)
XLA Modules:
  0.0 85.8 jit_solution(4349761220461596504)
XLA Ops:
  0.6 0.0 copy-start
  0.6 4.4 %all-to-all-start = ((bf16[4,144,256]{2,1,0:T(8,128)(2,1)}), bf16[4,144,256]{2,1,0:T(8,128)(2,1)S(1)}, u32[]{:S(2)}, u32[]{:S(2)}) async-start(bf16[4,144,256]{2,1,0:T(8,128)(2,1)} %bitcast.18), calls=%async_computation | async-start | bytes 589824 | tf_op jit(solution)/shard_map/all_to_all | solution.py:178
  5.1 0.1 fusion.13
  5.2 0.7 slice_bitcast_fusion.1
  5.9 0.1 copy.10
  6.0 0.1 tile.10
  6.1 1.3 %constant_dynamic-slice_fusion.1.weight_ref = f32[4,1024]{1,0:T(4,128)} fusion(f32[4,12288]{1,0:T(4,128)} %param.10, s32[]{:T(128)S(6)} %select_n.99), kind=kLoop, calls=%fused_computation.36 | loop fusion | bytes 32772 | tf_op jit(solution)/shard_map/dynamic_slice | solution.py:191
  7.4 1.3 %constant_dynamic-slice_fusion.2.index_ref = s32[4,1024]{1,0:T(4,128)} fusion(s32[4,12288]{1,0:T(4,128)} %param.9, s32[]{:T(128)S(6)} %select_n.99), kind=kLoop, calls=%fused_computation.37 | loop fusion | bytes 32772 | tf_op jit(solution)/shard_map/dynamic_slice | solution.py:190
  8.7 4.2 %all-to-all-done.own_ref = bf16[4,144,256]{2,1,0:T(8,128)(2,1)S(1)} async-done(((bf16[4,144,256]{2,1,0:T(8,128)(2,1)}), bf16[4,144,256]{2,1,0:T(8,128)(2,1)S(1)}, u32[]{:S(2)}, u32[]{:S(2)}) %all-to-all-start) | async-done | bytes 294944 | tf_op jit(solution)/shard_map/all_to_all | solution.py:178
  12.9 0.0 copy-start.1
  12.9 0.7 broadcast_in_dim.22
  13.6 15.2 %all-to-all-start.1 = ((f32[12,8,128]{2,1,0:T(8,128)}), f32[12,8,128]{2,1,0:T(8,128)S(1)}, u32[]{:S(2)}, u32[]{:S(2)}) async-start(f32[12,8,128]{2,1,0:T(8,128)} %broadcast_in_dim.22), calls=%async_computation.1 | async-start | bytes 98304 | tf_op jit(solution)/shard_map/all_to_all | solution.py:168
  28.8 1.3 %constant_dynamic-slice_fusion.mask_ref = s32[4,256]{1,0:T(4,128)} fusion(s32[48,256]{1,0:T(8,128)} %param.7, s32[]{:T(128)S(6)} %select_n.100), kind=kLoop, calls=%fused_computation.35 | loop fusion | bytes 8196 | tf_op jit(solution)/shard_map/dynamic_slice | solution.py:192
  30.1 3.9 %collective-permute-start = (bf16[4,144,256]{2,1,0:T(8,128)(2,1)S(1)}, bf16[4,144,256]{2,1,0:T(8,128)(2,1)S(1)}, u32[]{:S(2)}, u32[]{:S(2)}) collective-permute-start(bf16[4,144,256]{2,1,0:T(8,128)(2,1)S(1)} %all-to-all-done.own_ref), channel_id=1, source_target_pairs={{0,8},{2,10},{4,12},{6,14},{8,16},{10,18},{12,20},{14,22},{16,24},... | collective-permute-start | bytes 884744 | tf_op jit(solution)/shard_map/ppermute | solution.py:186
  34.0 5.3 %collective-permute-start.1 = (bf16[4,144,256]{2,1,0:T(8,128)(2,1)S(1)}, bf16[4,144,256]{2,1,0:T(8,128)(2,1)S(1)}, u32[]{:S(2)}, u32[]{:S(2)}) collective-permute-start(bf16[4,144,256]{2,1,0:T(8,128)(2,1)S(1)} %all-to-all-done.own_ref), channel_id=1, source_target_pairs={{8,0},{10,2},{12,4},{14,6},{16,8},{18,10},{20,12},{22,14},{24,16},... | collective-permute-start | bytes 884744 | tf_op jit(solution)/shard_map/ppermute | solution.py:187
  39.2 0.1 sine_multiply_fusion
  39.3 0.3 all-to-all-done.1
  39.6 0.6 broadcast_in_dim.23
  40.2 3.3 %all-to-all-start.2 = ((f32[4,8,128]{2,1,0:T(8,128)}), f32[4,8,128]{2,1,0:T(8,128)S(1)}, u32[]{:S(2)}, u32[]{:S(2)}) async-start(f32[4,8,128]{2,1,0:T(8,128)} %broadcast_in_dim.23), calls=%async_computation.2 | async-start | bytes 32768 | tf_op jit(solution)/shard_map/all_to_all | solution.py:173
  43.5 0.7 fusion.16
  44.2 4.6 %all-to-all-done.2.table_ref = f32[4,8,128]{2,1,0:T(8,128)S(1)} async-done(((f32[4,8,128]{2,1,0:T(8,128)}), f32[4,8,128]{2,1,0:T(8,128)S(1)}, u32[]{:S(2)}, u32[]{:S(2)}) %all-to-all-start.2) | async-done | bytes 16416 | tf_op jit(solution)/shard_map/all_to_all | solution.py:173
  48.8 0.0 copy-start.4
  48.8 0.6 copy-done.4
  49.4 1.9 %interpolate.1.fown_ref = f32[16,256]{1,0:T(8,128)} custom-call(f32[4,8,128]{2,1,0:T(8,128)} %copy-done.4, s32[4,1024]{1,0:T(4,128)} %constant_dynamic-slice_fusion.2.index_ref, f32[4,1024]{1,0:T(4,128)} %constant_dynamic-slice_fusion.1.weight_ref, s32[4,256]{1,0:T(4,128)} %constant_dynamic-slice_fusion.mask_ref), custom_call_target="tpu_custom_call" | custom-call | flops 2000000 | bytes 100000 | tf_op jit(solution)/shard_map/interpolate/pallas_call | solution.py:84
  51.3 2.6 %collective-permute-start.2 = (f32[16,256]{1,0:T(8,128)}, f32[16,256]{1,0:T(8,128)S(1)}, u32[]{:S(2)}, u32[]{:S(2)}) collective-permute-start(f32[16,256]{1,0:T(8,128)} %interpolate.1.fown_ref), channel_id=1, source_target_pairs={{0,8},{2,10},{4,12},{6,14},{8,16},{10,18},{12,20},{14,22},{16,24},... | collective-permute-start | bytes 49160 | tf_op jit(solution)/shard_map/ppermute | solution.py:194
  53.9 6.6 %collective-permute-start.3 = (f32[16,256]{1,0:T(8,128)}, f32[16,256]{1,0:T(8,128)S(1)}, u32[]{:S(2)}, u32[]{:S(2)}) collective-permute-start(f32[16,256]{1,0:T(8,128)} %interpolate.1.fown_ref), channel_id=1, source_target_pairs={{8,0},{10,2},{12,4},{14,6},{16,8},{18,10},{20,12},{22,14},{24,16},... | collective-permute-start | bytes 49160 | tf_op jit(solution)/shard_map/ppermute | solution.py:195
  60.5 0.0 collective-permute-done.2.fbelow_ref
  60.5 0.0 copy-start.5
  60.5 1.6 %collective-permute-done.3.fabove_ref = f32[16,256]{1,0:T(8,128)S(1)} collective-permute-done((f32[16,256]{1,0:T(8,128)}, f32[16,256]{1,0:T(8,128)S(1)}, u32[]{:S(2)}, u32[]{:S(2)}) %collective-permute-start.3) | collective-permute-done | bytes 16416 | tf_op jit(solution)/shard_map/ppermute | solution.py:195
  62.1 0.0 copy-start.6
  62.1 0.0 collective-permute-done.below_ref
  62.2 0.0 copy-start.2
  62.2 0.0 collective-permute-done.1.above_ref
  62.2 0.0 copy-start.3
  62.2 0.8 broadcast_in_dim.24.east_ref
  63.0 0.7 broadcast_in_dim.25.north_ref
  63.7 0.0 copy-done.1
  63.7 0.0 copy-done.5
  63.7 0.0 copy-done.6
  63.7 0.0 copy-done.2
  63.7 0.0 copy-done.3
  63.7 5.8 %propagate.1 = bf16[8,144,256]{2,1,0:T(8,128)(2,1)} custom-call(bf16[4,144,256]{2,1,0:T(8,128)(2,1)} %copy-done.2, bf16[4,144,256]{2,1,0:T(8,128)(2,1)} %copy-done.1, bf16[4,144,256]{2,1,0:T(8,128)(2,1)} %copy-done.3, f32[16,256]{1,0:T(8,128)} %copy-done.5, f32[16,256]{1,0:T(8,128)} %interpolate.1.fown_ref, f32[16,256]{1,0:T(8,128)} %copy-done.6, ...), custom_call_target="tpu_custom_call" | custom-call | flops 40000000 | bytes 1600000 | tf_op jit(solution)/shard_map/propagate/pallas_call | solution.py:141
  69.5 3.5 %all-to-all-start.3 = ((bf16[8,144,256]{2,1,0:T(8,128)(2,1)}), bf16[8,144,256]{2,1,0:T(8,128)(2,1)S(1)}, u32[]{:S(2)}, u32[]{:S(2)}) async-start(bf16[8,144,256]{2,1,0:T(8,128)(2,1)} %propagate.1), calls=%async_computation.3 | async-start | bytes 1179648 | tf_op jit(solution)/shard_map/all_to_all | solution.py:204
  73.0 0.1 multiply_convert_fusion.2
  73.1 10.6 %all-to-all-done.3 = bf16[8,144,256]{2,1,0:T(8,128)(2,1)S(1)} async-done(((bf16[8,144,256]{2,1,0:T(8,128)(2,1)}), bf16[8,144,256]{2,1,0:T(8,128)(2,1)S(1)}, u32[]{:S(2)}, u32[]{:S(2)}) %all-to-all-start.3) | async-done | bytes 589856 | tf_op jit(solution)/shard_map/all_to_all | solution.py:204
  83.7 0.8 fusion.23
  84.5 0.0 copy-done
  84.5 1.3 %multiply_convert_fusion = bf16[576,256]{1,0:T(8,128)(2,1)} fusion(bf16[1152,256]{1,0:T(8,128)(2,1)S(1)} %bitcast.17, s32[]{:T(128)S(6)} %select_n.104, f32[256]{0:T(256)S(1)} %bitcast.20, bf16[576,1152]{1,0:T(8,128)(2,1)S(1)} %copy-done), kind=kOutput, calls=%fused_computation.1 | convolution fusion | flops 340475904 | bytes 2507780 | tf_op jit(solution)/shard_map/dot_general | solution.py:210
  (8 shorter events, 0.1 us)
Async XLA Ops:
  0.6 83.9 %copy-start = (bf16[576,1152]{1,0:T(8,128)(2,1)S(1)}, bf16[576,1152]{1,0:T(8,128)(2,1)}, u32[]{:S(2)}) copy-start(bf16[576,1152]{1,0:T(8,128)(2,1)} %param.11) | copy-start | bytes 3981316
  0.6 12.3 %all-to-all-start = ((bf16[4,144,256]{2,1,0:T(8,128)(2,1)}), bf16[4,144,256]{2,1,0:T(8,128)(2,1)S(1)}, u32[]{:S(2)}, u32[]{:S(2)}) async-start(bf16[4,144,256]{2,1,0:T(8,128)(2,1)} %bitcast.18), calls=%async_computation | async-start | bytes 589824 | tf_op jit(solution)/shard_map/all_to_all | solution.py:178
  12.9 50.7 %copy-start.1 = (bf16[4,144,256]{2,1,0:T(8,128)(2,1)}, bf16[4,144,256]{2,1,0:T(8,128)(2,1)S(1)}, u32[]{:S(2)}) copy-start(bf16[4,144,256]{2,1,0:T(8,128)(2,1)S(1)} %all-to-all-done.own_ref) | copy-start | bytes 884740
  13.6 26.0 %all-to-all-start.1 = ((f32[12,8,128]{2,1,0:T(8,128)}), f32[12,8,128]{2,1,0:T(8,128)S(1)}, u32[]{:S(2)}, u32[]{:S(2)}) async-start(f32[12,8,128]{2,1,0:T(8,128)} %broadcast_in_dim.22), calls=%async_computation.1 | async-start | bytes 98304 | tf_op jit(solution)/shard_map/all_to_all | solution.py:168
  30.1 32.1 %collective-permute-start = (bf16[4,144,256]{2,1,0:T(8,128)(2,1)S(1)}, bf16[4,144,256]{2,1,0:T(8,128)(2,1)S(1)}, u32[]{:S(2)}, u32[]{:S(2)}) collective-permute-start(bf16[4,144,256]{2,1,0:T(8,128)(2,1)S(1)} %all-to-all-done.own_ref), channel_id=1, source_target_pairs={{0,8},{2,10},{4,12},{6,14},{8,16},{10,18},{12,20},{14,22},{16,24},... | collective-permute-start | bytes 884744 | tf_op jit(solution)/shard_map/ppermute | solution.py:186
  34.0 28.2 %collective-permute-start.1 = (bf16[4,144,256]{2,1,0:T(8,128)(2,1)S(1)}, bf16[4,144,256]{2,1,0:T(8,128)(2,1)S(1)}, u32[]{:S(2)}, u32[]{:S(2)}) collective-permute-start(bf16[4,144,256]{2,1,0:T(8,128)(2,1)S(1)} %all-to-all-done.own_ref), channel_id=1, source_target_pairs={{8,0},{10,2},{12,4},{14,6},{16,8},{18,10},{20,12},{22,14},{24,16},... | collective-permute-start | bytes 884744 | tf_op jit(solution)/shard_map/ppermute | solution.py:187
  40.2 8.6 %all-to-all-start.2 = ((f32[4,8,128]{2,1,0:T(8,128)}), f32[4,8,128]{2,1,0:T(8,128)S(1)}, u32[]{:S(2)}, u32[]{:S(2)}) async-start(f32[4,8,128]{2,1,0:T(8,128)} %broadcast_in_dim.23), calls=%async_computation.2 | async-start | bytes 32768 | tf_op jit(solution)/shard_map/all_to_all | solution.py:173
  48.8 0.6 copy-start.4
  51.3 9.2 %collective-permute-start.2 = (f32[16,256]{1,0:T(8,128)}, f32[16,256]{1,0:T(8,128)S(1)}, u32[]{:S(2)}, u32[]{:S(2)}) collective-permute-start(f32[16,256]{1,0:T(8,128)} %interpolate.1.fown_ref), channel_id=1, source_target_pairs={{0,8},{2,10},{4,12},{6,14},{8,16},{10,18},{12,20},{14,22},{16,24},... | collective-permute-start | bytes 49160 | tf_op jit(solution)/shard_map/ppermute | solution.py:194
  53.9 8.2 %collective-permute-start.3 = (f32[16,256]{1,0:T(8,128)}, f32[16,256]{1,0:T(8,128)S(1)}, u32[]{:S(2)}, u32[]{:S(2)}) collective-permute-start(f32[16,256]{1,0:T(8,128)} %interpolate.1.fown_ref), channel_id=1, source_target_pairs={{8,0},{10,2},{12,4},{14,6},{16,8},{18,10},{20,12},{22,14},{24,16},... | collective-permute-start | bytes 49160 | tf_op jit(solution)/shard_map/ppermute | solution.py:195
  60.5 3.1 %copy-start.5 = (f32[16,256]{1,0:T(8,128)}, f32[16,256]{1,0:T(8,128)S(1)}, u32[]{:S(2)}) copy-start(f32[16,256]{1,0:T(8,128)S(1)} %collective-permute-done.2.fbelow_ref) | copy-start | bytes 49156
  62.1 1.5 %copy-start.6 = (f32[16,256]{1,0:T(8,128)}, f32[16,256]{1,0:T(8,128)S(1)}, u32[]{:S(2)}) copy-start(f32[16,256]{1,0:T(8,128)S(1)} %collective-permute-done.3.fabove_ref) | copy-start | bytes 49156
  62.2 1.5 %copy-start.2 = (bf16[4,144,256]{2,1,0:T(8,128)(2,1)}, bf16[4,144,256]{2,1,0:T(8,128)(2,1)S(1)}, u32[]{:S(2)}) copy-start(bf16[4,144,256]{2,1,0:T(8,128)(2,1)S(1)} %collective-permute-done.below_ref) | copy-start | bytes 884740
  62.2 1.5 %copy-start.3 = (bf16[4,144,256]{2,1,0:T(8,128)(2,1)}, bf16[4,144,256]{2,1,0:T(8,128)(2,1)S(1)}, u32[]{:S(2)}) copy-start(bf16[4,144,256]{2,1,0:T(8,128)(2,1)S(1)} %collective-permute-done.1.above_ref) | copy-start | bytes 884740
  69.5 14.2 %all-to-all-start.3 = ((bf16[8,144,256]{2,1,0:T(8,128)(2,1)}), bf16[8,144,256]{2,1,0:T(8,128)(2,1)S(1)}, u32[]{:S(2)}, u32[]{:S(2)}) async-start(bf16[8,144,256]{2,1,0:T(8,128)(2,1)} %propagate.1), calls=%async_computation.3 | async-start | bytes 1179648 | tf_op jit(solution)/shard_map/all_to_all | solution.py:204

commit v2 on v1

--- a/solution.py
+++ b/solution.py
@@ -6,6 +6,7 @@
 from jax.experimental import pallas as pl
 from jax.experimental.pallas import tpu as pltpu
 from jax.sharding import PartitionSpec as P
+
 
 NFREQ = 32
 NDIR = 36
@@ -44,30 +45,37 @@
     return jnp.concatenate([eastward, northward], 0).astype(jnp.bfloat16)
 
 
-def interpolate_body(table_ref, index_ref, weight_ref, mask_ref, out_ref):
-    rows, cols = mask_ref.shape
+def interpolate_body(
+    place_ref, gathered_ref, index_ref, weight_ref, mask_ref, out_ref
+):
+    groups = gathered_ref.shape[0]
+    cols = mask_ref.shape[1]
+    rows = ROWS
     row_ids = lax.broadcasted_iota(jnp.int32, (OCEAN_ROWS, 128), 0)
-    tables = [table_ref[q] for q in range(4)]
+    tables = []
+    for part in range(groups // 4):
+        pieces = [gathered_ref[4 * part + i] for i in range(4)]
+        tables.append((pieces[0] + pieces[1]) + (pieces[2] + pieces[3]))
     for chunk in range(rows * cols // 128):
         lanes = slice(chunk * 128, chunk * 128 + 128)
         cells = index_ref[:, lanes]
         shares = weight_ref[:, lanes]
         row_of = (cells * 5462) >> 20
         column_of = cells - row_of * OCEAN_COLS
-        lane_of = (column_of >> 4) * 8 + (column_of & 3)
-        quarter_of = (column_of >> 2) & 3
+        lane_of = ((column_of & 63) >> 2) * 8 + (column_of & 3)
+        part_of = column_of >> 6
         totals = [jnp.zeros((OCEAN_ROWS, 128), jnp.float32) for _ in range(2)]
         for corner in range(4):
             row_b = jnp.broadcast_to(row_of[corner : corner + 1], (OCEAN_ROWS, 128))
             lane_b = jnp.broadcast_to(lane_of[corner : corner + 1], (OCEAN_ROWS, 128))
-            quarter_b = jnp.broadcast_to(quarter_of[corner : corner + 1], (OCEAN_ROWS, 128))
+            part_b = jnp.broadcast_to(part_of[corner : corner + 1], (OCEAN_ROWS, 128))
             share_b = jnp.broadcast_to(shares[corner : corner + 1], (OCEAN_ROWS, 128))
             weight = jnp.where(row_b == row_ids, share_b, 0.0)
             for c in range(2):
                 picked = jnp.take_along_axis(tables[0], lane_b + 4 * c, axis=1)
-                for q in range(1, 4):
-                    other = jnp.take_along_axis(tables[q], lane_b + 4 * c, axis=1)
-                    picked = jnp.where(quarter_b == q, other, picked)
+                for part in range(1, len(tables)):
+                    other = jnp.take_along_axis(tables[part], lane_b + 4 * c, axis=1)
+                    picked = jnp.where(part_b == part, other, picked)
                 totals[c] += picked * weight
         row = chunk * 128 // cols
         spot = slice(chunk * 128 % cols, chunk * 128 % cols + 128)
@@ -75,27 +83,48 @@
             out_ref[c * rows + row : c * rows + row + 1, spot] = courant * jnp.sum(
                 totals[c], axis=0, keepdims=True
             )
-    out_ref[2 * rows : 3 * rows, :] = mask_ref[...].astype(jnp.float32)
+    upper = place_ref[pl.program_id(0)] % 2 == 1
+    mask = jnp.where(upper, mask_ref[rows : 2 * rows, :], mask_ref[0:rows, :])
+    out_ref[2 * rows : 3 * rows, :] = mask.astype(jnp.float32)
     out_ref[3 * rows :, :] = jnp.zeros((rows, cols), jnp.float32)
 
 
-def interpolate(table, cells, shares, mask):
-    rows, cols = mask.shape
+def interpolate(places, gathered, remap_index, remap_weights, wet_mask):
+    count = places.shape[0]
+    cols = wet_mask.shape[1]
+    block = ROWS * cols
     return pl.pallas_call(
         interpolate_body,
-        out_shape=jax.ShapeDtypeStruct((4 * rows, cols), jnp.float32),
-        in_specs=[pl.BlockSpec(memory_space=pltpu.VMEM)] * 4,
-        out_specs=pl.BlockSpec(memory_space=pltpu.VMEM),
-        cost_estimate=pl.CostEstimate(flops=2_000_000, bytes_accessed=100_000, transcendentals=0),
+        grid_spec=pltpu.PrefetchScalarGridSpec(
+            num_scalar_prefetch=1,
+            grid=(count,),
+            in_specs=[
+                pl.BlockSpec(gathered.shape, lambda i, place: (0, 0, 0)),
+                pl.BlockSpec((4, block), lambda i, place: (0, place[i])),
+                pl.BlockSpec((4, block), lambda i, place: (0, place[i])),
+                pl.BlockSpec((2 * ROWS, cols), lambda i, place: (place[i] // 2, 0)),
+            ],
+            out_specs=pl.BlockSpec((4 * ROWS, cols), lambda i, place: (i, 0)),
+        ),
+        out_shape=jax.ShapeDtypeStruct((count * 4 * ROWS, cols), jnp.float32),
+        compiler_params=pltpu.CompilerParams(vmem_limit_bytes=4 << 20),
+        cost_estimate=pl.CostEstimate(
+            flops=2_000_000 * count, bytes_accessed=100_000 * count, transcendentals=0
+        ),
         name="interpolate",
-    )(table, cells, shares, mask)
+    )(places, gathered, remap_index, remap_weights, wet_mask)
 
 
 def propagate_body(
-    below_ref, own_ref, above_ref, fbelow_ref, fown_ref, fabove_ref, east_ref, north_ref, out_ref
+    edge_ref, below_ref, own_ref, above_ref, fown_ref, fbeside_ref, fother_ref, east_ref, north_ref,
+    out_ref, fbelow_ref, fabove_ref,
 ):
     rows, bins, cols = own_ref.shape
     tile = 16
+    deep = 4 * rows
+    fother = fother_ref[...]
+    fbelow_ref[...] = jnp.where(edge_ref[0] == 1, fother, fbeside_ref[0:deep, :])
+    fabove_ref[...] = jnp.where(edge_ref[1] == 1, fother, fbeside_ref[deep:, :])
 
     def one_tile(t, carry):
         spot = pl.ds(pl.multiple_of(t * tile, tile), tile)
@@ -136,24 +165,26 @@
     lax.fori_loop(0, bins // tile, one_tile, 0)
 
 
-def propagate(below, own, above, fbelow, fown, fabove, east, north):
+def propagate(edges, below, own, above, fown, fbeside, fother, east, north):
     rows, bins, cols = own.shape
     return pl.pallas_call(
         propagate_body,
         out_shape=jax.ShapeDtypeStruct((2 * rows, bins, cols), jnp.bfloat16),
-        in_specs=[pl.BlockSpec(memory_space=pltpu.VMEM)] * 8,
+        in_specs=[pl.BlockSpec(memory_space=pltpu.SMEM)]
+        + [pl.BlockSpec(memory_space=pltpu.VMEM)] * 8,
         out_specs=pl.BlockSpec(memory_space=pltpu.VMEM),
+        scratch_shapes=[pltpu.VMEM((4 * rows, cols), jnp.float32)] * 2,
+        compiler_params=pltpu.CompilerParams(vmem_limit_bytes=8 << 20),
         cost_estimate=pl.CostEstimate(flops=40_000_000, bytes_accessed=1_600_000, transcendentals=0),
         name="propagate",
-    )(below, own, above, fbelow, fown, fabove, east, north)
-
-
-def per_device(spectrum, wet_mask, currents, remap_index, remap_weights, source_matrix):
+    )(edges, below, own, above, fown, fbeside, fother, east, north)
+
+
+def step(spectrum, wet_mask, currents, remap_index, remap_weights, source_matrix):
     wide_index = lax.axis_index("wide")
     comp_index = lax.axis_index("comp")
     strips, wides = lax.axis_size("strip"), lax.axis_size("wide")
     comps = lax.axis_size("comp")
-    lat_rows, lon_cells = wet_mask.shape
     local_bins, points = spectrum.shape
     groups = wides // ROWS
     group_index = wide_index // ROWS
@@ -164,20 +195,18 @@
 
     lane = jnp.arange(128, dtype=jnp.int32)
     ours = jnp.concatenate([currents[0], currents[1]], axis=1)
-    ours = jnp.where((lane // 8 == group_index)[None, :], jnp.tile(ours, (1, 16)), 0.0)
-    along = lax.all_to_all(
-        jnp.broadcast_to(ours[None], (groups, OCEAN_ROWS, 128)),
-        "wide", split_axis=0, concat_axis=0, tiled=True, axis_index_groups=far,
-    )
-    along = jnp.sum(along, 0)
-    table = lax.all_to_all(
-        jnp.broadcast_to(along[None], (ROWS, OCEAN_ROWS, 128)),
-        "wide", split_axis=0, concat_axis=0, tiled=True, axis_index_groups=near,
-    )
-
+    ours = jnp.where((lane // 8 == wide_index % 16)[None, :], jnp.tile(ours, (1, 16)), 0.0)
+    table = ours
+    for turn in range(1, ROWS):
+        swap = [(i, i - i % ROWS + (i % ROWS ^ turn)) for i in range(wides)]
+        table = table + lax.ppermute(ours, "wide", swap)
     own = lax.all_to_all(
         spectrum.reshape(ROWS, share, points),
         "wide", split_axis=0, concat_axis=0, tiled=True, axis_index_groups=near,
+    )
+    table = lax.all_to_all(
+        jnp.broadcast_to(table[None], (groups, OCEAN_ROWS, 128)),
+        "wide", split_axis=0, concat_axis=0, tiled=True, axis_index_groups=far,
     )
     total = strips * wides
     upward = [(i, i + ROWS) for i in range(total - ROWS)]
@@ -185,18 +214,17 @@
     chain = ("strip", "wide")
     below = lax.ppermute(own, chain, upward)
     above = lax.ppermute(own, chain, downward)
-
-    first = group_index * ROWS * lon_cells
-    cells = lax.dynamic_slice_in_dim(remap_index, first, ROWS * lon_cells, 1)
-    shares = lax.dynamic_slice_in_dim(remap_weights, first, ROWS * lon_cells, 1)
-    mask = lax.dynamic_slice_in_dim(wet_mask, group_index * ROWS, ROWS, 0)
-    fown = interpolate(table, cells, shares, mask)
-    fbelow = lax.ppermute(fown, chain, upward)
-    fabove = lax.ppermute(fown, chain, downward)
+    args = (table, remap_index, remap_weights, wet_mask)
+    fown = interpolate(group_index.reshape(1), *args)
+    crossing = [(s * wides + wides - ROWS + i, (s + 1) * wides + i) for s in range(strips - 1) for i in range(ROWS)]
+    fother = lax.ppermute(fown, chain, crossing + [(b, a) for a, b in crossing])
+    beside = jnp.stack([jnp.maximum(group_index - 1, 0), jnp.minimum(group_index + 1, groups - 1)])
+    fbeside = interpolate(beside, *args)
+    edges = jnp.stack([group_index == 0, group_index == groups - 1]).astype(jnp.int32)
 
     first_bin = comp_index * local_bins + member * share
     east, north = bin_speeds(first_bin, share)
-    spread = propagate(below, own, above, fbelow, fown, fabove, east, north)
+    spread = propagate(edges, below, own, above, fown, fbeside, fother, east, north)
 
     both = [
         [(ROWS * g + i) * comps + k for k in range(comps) for i in range(ROWS)] for g in range(groups)
@@ -227,7 +255,7 @@
         P("comp", None),
     )
     return jax.shard_map(
-        per_device,
+        step,
         mesh=mesh,
         in_specs=placed,
         out_specs=(P("comp", ("strip", "wide")), P(None, "comp", ("strip", "wide"))),

time: 86.7 us -> 84 us (0.969)
  local copies, waits for them, and re-layouts: 8.23 us -> 4.44 us
  waiting for transfers between devices: 21.3 us -> 23.8 us
  starting transfers between devices: 44.7 us -> 43.8 us
    dynamic_slice x3 -> x0, local copies, waits for them, and re-layouts: 3.93 us -> none  [the longest x1 1.32 us: per_device(): shares = lax.dynamic_slice_in_dim(remap_weights, first, ROWS * lon_cells, 1)]
    all_to_all x4 -> x3, starting transfers between devices: 26.4 us -> 23 us  [the longest x1 15.2 us: step(): lax.all_to_all(jnp.broadcast_to(table[None], (groups, OCEAN_ROWS, 128)),...]
    ppermute x4 -> x6, waiting for transfers between devices: 1.61 us -> 4.73 us  [the longest x1 4.72 us: step(): fother = lax.ppermute(fown, chain, crossing + [(b, a) for a, b in crossing])]
    ppermute x4 -> x6, starting transfers between devices: 18.3 us -> 20.8 us  [the longest x3 9.09 us: step(): table = table + lax.ppermute(ours, 'wide', swap)]
    unnamed x14, local copies, waits for them, and re-layouts: 0.64 us -> 2.68 us
    all_to_all x4 -> x3, waiting for transfers between devices: 19.7 us -> 19.1 us  [the longest x1 10.6 us: step(): lax.all_to_all(spread, ('wide', 'comp'), split_axis=0, concat_axis=0, til...]
    pallas_call x1 -> x2, Pallas kernels: 1.91 us -> 2.06 us  [interpolate(): pl.pallas_call(interpolate_body, grid_spec=pltpu.PrefetchScalarGridSpec(n...]
  transfers between devices with their start and end apart: 8 -> 9, of which waited for: 5 -> 4; matrix products, arithmetic and copies ran while one was open for 7% -> 1% of each run, Pallas kernels for 2% -> 2%
where the time goes in v2:
time: 84 us; the launch traced here: 83.3 us
  starting transfers between devices  43.8 us (52%)
  waiting for transfers between devices  23.8 us (28%)
  Pallas kernels  7.17 us (9%)
  local copies, waits for them, and re-layouts  4.44 us (5%)
  matrix products  2.11 us (3%)
  other arithmetic  1.13 us (1%)
  between operations  0.85 us (1%)
    all_to_all x1, starting transfers between devices, step(): lax.all_to_all(jnp.broadcast_to(table[None], (groups, OCEAN_ROWS, 128)),...  15.2 us
    all_to_all x1, waiting for transfers between devices, step(): lax.all_to_all(spread, ('wide', 'comp'), split_axis=0, concat_axis=0, til...  10.6 us
    ppermute x3, starting transfers between devices, step(): table = table + lax.ppermute(ours, 'wide', swap)  9.09 us
    all_to_all x1, waiting for transfers between devices, step(): lax.all_to_all(spectrum.reshape(ROWS, share, points), 'wide', split_axis=...  7.02 us
    ppermute x1, starting transfers between devices, step(): above = lax.ppermute(own, chain, downward)  5.28 us
    pallas_call x1, Pallas kernels, propagate(): pl.pallas_call(propagate_body, out_shape=jax.ShapeDtypeStruct((2 * rows,...  5.11 us
    ppermute x1, waiting for transfers between devices, step(): fother = lax.ppermute(fown, chain, crossing + [(b, a) for a, b in crossing])  4.72 us
    all_to_all x1, starting transfers between devices, step(): lax.all_to_all(spectrum.reshape(ROWS, share, points), 'wide', split_axis=...  4.3 us
  transfers between devices with their start and end apart: 9, of which 4 were waited for; matrix products, arithmetic and copies ran while one was open for 1% of the time, Pallas kernels for 2%

profile of v2, /device:TPU:32, one launch (start us, length us, event | category | flops | bytes accessed | tf_op | source)
XLA Modules:
  0.0 83.3 jit_solution(6330988846557211776)
XLA Ops:
  0.6 0.0 copy-start
  0.6 0.0 copy-start.6
  0.7 0.0 copy-start.4
  0.7 0.0 copy-start.2
  0.7 0.8 slice_bitcast_fusion.1
  1.5 0.1 copy.9
  1.6 0.1 tile.10
  1.7 1.9 %collective-permute-start.2 = (f32[8,128]{1,0:T(8,128)S(1)}, f32[8,128]{1,0:T(8,128)S(1)}, u32[]{:S(2)}, u32[]{:S(2)}) collective-permute-start(f32[8,128]{1,0:T(8,128)S(1)} %broadcast_select_fusion), channel_id=1, source_target_pairs={{0,2},{2,0},{4,6},{6,4},{8,10},{10,8},{12,14},{14,12},{16,18},{18,... | collective-permute-start | bytes 12296 | tf_op jit(solution)/shard_map/ppermute | solution.py:202
  3.7 4.9 %collective-permute-start.3 = (f32[8,128]{1,0:T(8,128)S(1)}, f32[8,128]{1,0:T(8,128)S(1)}, u32[]{:S(2)}, u32[]{:S(2)}) collective-permute-start(f32[8,128]{1,0:T(8,128)S(1)} %broadcast_select_fusion), channel_id=1, source_target_pairs={{0,4},{2,6},{4,0},{6,2},{8,12},{10,14},{12,8},{14,10},{16,20},{18,... | collective-permute-start | bytes 12296 | tf_op jit(solution)/shard_map/ppermute | solution.py:202
  8.6 2.2 %collective-permute-start.4 = (f32[8,128]{1,0:T(8,128)S(1)}, f32[8,128]{1,0:T(8,128)S(1)}, u32[]{:S(2)}, u32[]{:S(2)}) collective-permute-start(f32[8,128]{1,0:T(8,128)S(1)} %broadcast_select_fusion), channel_id=1, source_target_pairs={{0,6},{2,4},{4,2},{6,0},{8,14},{10,12},{12,10},{14,8},{16,22},{18,... | collective-permute-start | bytes 12296 | tf_op jit(solution)/shard_map/ppermute | solution.py:202
  10.8 4.3 %all-to-all-start = ((bf16[4,144,256]{2,1,0:T(8,128)(2,1)}), bf16[4,144,256]{2,1,0:T(8,128)(2,1)S(1)}, u32[]{:S(2)}, u32[]{:S(2)}) async-start(bf16[4,144,256]{2,1,0:T(8,128)(2,1)} %bitcast.23), calls=%async_computation | async-start | bytes 589824 | tf_op jit(solution)/shard_map/all_to_all | solution.py:203
  15.2 0.1 sine_multiply_fusion
  15.2 0.7 dynamic-slice_convert_fusion
  15.9 0.0 collective-permute-done.2
  16.0 0.0 collective-permute-done.3
  16.0 0.0 collective-permute-done.4
  16.0 7.0 %all-to-all-done.own_ref = bf16[4,144,256]{2,1,0:T(8,128)(2,1)S(1)} async-done(((bf16[4,144,256]{2,1,0:T(8,128)(2,1)}), bf16[4,144,256]{2,1,0:T(8,128)(2,1)S(1)}, u32[]{:S(2)}, u32[]{:S(2)}) %all-to-all-start) | async-done | bytes 294944 | tf_op jit(solution)/shard_map/all_to_all | solution.py:203
  23.0 0.6 broadcast_in_dim.20
  23.6 15.2 %all-to-all-start.1 = ((f32[12,8,128]{2,1,0:T(8,128)}), f32[12,8,128]{2,1,0:T(8,128)S(1)}, u32[]{:S(2)}, u32[]{:S(2)}) async-start(f32[12,8,128]{2,1,0:T(8,128)} %broadcast_in_dim.20), calls=%async_computation.1 | async-start | bytes 98304 | tf_op jit(solution)/shard_map/all_to_all | solution.py:207
  38.8 3.9 %collective-permute-start = (bf16[4,144,256]{2,1,0:T(8,128)(2,1)S(1)}, bf16[4,144,256]{2,1,0:T(8,128)(2,1)S(1)}, u32[]{:S(2)}, u32[]{:S(2)}) collective-permute-start(bf16[4,144,256]{2,1,0:T(8,128)(2,1)S(1)} %all-to-all-done.own_ref), channel_id=1, source_target_pairs={{0,8},{2,10},{4,12},{6,14},{8,16},{10,18},{12,20},{14,22},{16,24},... | collective-permute-start | bytes 884744 | tf_op jit(solution)/shard_map/ppermute | solution.py:215
  42.7 5.3 %collective-permute-start.1 = (bf16[4,144,256]{2,1,0:T(8,128)(2,1)S(1)}, bf16[4,144,256]{2,1,0:T(8,128)(2,1)S(1)}, u32[]{:S(2)}, u32[]{:S(2)}) collective-permute-start(bf16[4,144,256]{2,1,0:T(8,128)(2,1)S(1)} %all-to-all-done.own_ref), channel_id=1, source_target_pairs={{8,0},{10,2},{12,4},{14,6},{16,8},{18,10},{20,12},{22,14},{24,16},... | collective-permute-start | bytes 884744 | tf_op jit(solution)/shard_map/ppermute | solution.py:216
  48.0 0.1 pad_add_fusion.place_ref
  48.1 0.1 fusion.13
  48.1 1.5 %all-to-all-done.1.gathered_ref = f32[12,8,128]{2,1,0:T(8,128)S(1)} async-done(((f32[12,8,128]{2,1,0:T(8,128)}), f32[12,8,128]{2,1,0:T(8,128)S(1)}, u32[]{:S(2)}, u32[]{:S(2)}) %all-to-all-start.1) | async-done | bytes 49184 | tf_op jit(solution)/shard_map/all_to_all | solution.py:207
  49.6 0.0 copy-start.1
  49.6 0.9 %copy-done.1 = s32[4,12288]{1,0:T(4,128)S(1)} copy-done((s32[4,12288]{1,0:T(4,128)S(1)}, s32[4,12288]{1,0:T(4,128)}, u32[]{:S(2)}) %copy-start.1) | copy-done | bytes 196632
  50.6 0.0 copy-start.3
  50.6 0.9 %copy-done.3 = f32[4,12288]{1,0:T(4,128)S(1)} copy-done((f32[4,12288]{1,0:T(4,128)S(1)}, f32[4,12288]{1,0:T(4,128)}, u32[]{:S(2)}) %copy-start.3) | copy-done | bytes 196632
  51.5 0.8 copy-done.5
  52.3 0.5 interpolate.2.fown_ref
  52.8 2.6 %collective-permute-start.5 = (f32[16,256]{1,0:T(8,128)S(1)}, f32[16,256]{1,0:T(8,128)S(1)}, u32[]{:S(2)}, u32[]{:S(2)}) collective-permute-start(f32[16,256]{1,0:T(8,128)S(1)} %interpolate.2.fown_ref), channel_id=1, source_target_pairs={{88,96},{90,98},{92,100},{94,102},{184,192},{186,194},{188,196},{1... | collective-permute-start | bytes 49160 | tf_op jit(solution)/shard_map/ppermute | solution.py:220
  55.4 0.1 add_convert_fusion.edge_ref
  55.4 0.0 copy-done.6
  55.4 0.0 copy-done.4
  55.5 0.0 copy-done.2
  55.5 1.6 %interpolate.3.fbeside_ref = f32[32,256]{1,0:T(8,128)S(1)} custom-call(s32[2]{0:T(128)S(1)} %pad_add_fusion.place_ref, f32[12,8,128]{2,1,0:T(8,128)S(1)} %all-to-all-done.1.gathered_ref, s32[4,12288]{1,0:T(4,128)S(1)} %copy-done.2, f32[4,12288]{1,0:T(4,128)S(1)} %copy-done.4, s32[48,256]{1,0:T(8,128)S(1)} %copy-done.6), custom_call_target="tpu_custom_call" | custom-call | flops 4000000 | bytes 200000 | tf_op jit(solution)/shard_map/interpolate/pallas_call | solution.py:96
  57.0 4.7 %collective-permute-done.5.fother_ref = f32[16,256]{1,0:T(8,128)S(1)} collective-permute-done((f32[16,256]{1,0:T(8,128)S(1)}, f32[16,256]{1,0:T(8,128)S(1)}, u32[]{:S(2)}, u32[]{:S(2)}) %collective-permute-start.5) | collective-permute-done | bytes 16416 | tf_op jit(solution)/shard_map/ppermute | solution.py:220
  61.7 0.0 collective-permute-done.below_ref
  61.7 0.0 collective-permute-done.1.above_ref
  61.8 0.1 broadcast_in_dim.21.east_ref
  61.8 0.1 broadcast_in_dim.22.north_ref
  61.9 5.1 %propagate.1 = bf16[8,144,256]{2,1,0:T(8,128)(2,1)} custom-call(s32[2]{0:T(128)S(1)} %add_convert_fusion.edge_ref, bf16[4,144,256]{2,1,0:T(8,128)(2,1)S(1)} %collective-permute-done.below_ref, bf16[4,144,256]{2,1,0:T(8,128)(2,1)S(1)} %all-to-all-done.own_ref, bf16[4,144,256]{2,1,0:T(8,128)(2,1)S(1)} %collective-permute-done.1.above_ref, ...), custom_call_target="tpu_custom_call" | custom-call | flops 40000000 | bytes 1600000 | tf_op jit(solution)/shard_map/propagate/pallas_call | solution.py:170
  67.0 3.5 %all-to-all-start.2 = ((bf16[8,144,256]{2,1,0:T(8,128)(2,1)}), bf16[8,144,256]{2,1,0:T(8,128)(2,1)S(1)}, u32[]{:S(2)}, u32[]{:S(2)}) async-start(bf16[8,144,256]{2,1,0:T(8,128)(2,1)} %propagate.1), calls=%async_computation.2 | async-start | bytes 1179648 | tf_op jit(solution)/shard_map/all_to_all | solution.py:232
  70.6 0.1 multiply_convert_fusion.2
  70.7 10.6 %all-to-all-done.2 = bf16[8,144,256]{2,1,0:T(8,128)(2,1)S(1)} async-done(((bf16[8,144,256]{2,1,0:T(8,128)(2,1)}), bf16[8,144,256]{2,1,0:T(8,128)(2,1)S(1)}, u32[]{:S(2)}, u32[]{:S(2)}) %all-to-all-start.2) | async-done | bytes 589856 | tf_op jit(solution)/shard_map/all_to_all | solution.py:232
  81.2 0.8 %fusion.22 = f32[2,16,256]{2,1,0:T(8,128)} fusion(bf16[2,16,1152]{2,1,0:T(8,128)(2,1)S(1)} %bitcast.24, bf16[1152,256,1]{1,0,2:T(8,128)(2,1)S(1)} %bitcast.21), kind=kOutput, calls=%fused_computation.53 | convolution fusion | flops 18874368 | bytes 696320 | tf_op jit(solution)/shard_map/dot_general | solution.py:239
  82.1 0.0 copy-done
  82.1 1.3 %multiply_convert_fusion = bf16[576,256]{1,0:T(8,128)(2,1)} fusion(bf16[1152,256]{1,0:T(8,128)(2,1)S(1)} %bitcast.22, s32[]{:T(128)S(6)} %select_n.96, f32[256]{0:T(256)S(1)} %bitcast.25, bf16[576,1152]{1,0:T(8,128)(2,1)S(1)} %copy-done), kind=kOutput, calls=%fused_computation.1 | convolution fusion | flops 340475904 | bytes 2507780 | tf_op jit(solution)/shard_map/dot_general | solution.py:238
  (9 shorter events, 0.1 us)
Async XLA Ops:
  0.6 81.4 %copy-start = (bf16[576,1152]{1,0:T(8,128)(2,1)S(1)}, bf16[576,1152]{1,0:T(8,128)(2,1)}, u32[]{:S(2)}) copy-start(bf16[576,1152]{1,0:T(8,128)(2,1)} %param.11) | copy-start | bytes 3981316
  0.6 54.8 %copy-start.6 = (s32[48,256]{1,0:T(8,128)S(1)}, s32[48,256]{1,0:T(8,128)}, u32[]{:S(2)}) copy-start(s32[48,256]{1,0:T(8,128)} %mask_ref.3) | copy-start | bytes 147460
  0.7 54.8 %copy-start.4 = (f32[4,12288]{1,0:T(4,128)S(1)}, f32[4,12288]{1,0:T(4,128)}, u32[]{:S(2)}) copy-start(f32[4,12288]{1,0:T(4,128)} %weight_ref.3) | copy-start | bytes 589828
  0.7 54.8 %copy-start.2 = (s32[4,12288]{1,0:T(4,128)S(1)}, s32[4,12288]{1,0:T(4,128)}, u32[]{:S(2)}) copy-start(s32[4,12288]{1,0:T(4,128)} %index_ref.3) | copy-start | bytes 589828
  1.7 14.2 %collective-permute-start.2 = (f32[8,128]{1,0:T(8,128)S(1)}, f32[8,128]{1,0:T(8,128)S(1)}, u32[]{:S(2)}, u32[]{:S(2)}) collective-permute-start(f32[8,128]{1,0:T(8,128)S(1)} %broadcast_select_fusion), channel_id=1, source_target_pairs={{0,2},{2,0},{4,6},{6,4},{8,10},{10,8},{12,14},{14,12},{16,18},{18,... | collective-permute-start | bytes 12296 | tf_op jit(solution)/shard_map/ppermute | solution.py:202
  3.7 12.3 %collective-permute-start.3 = (f32[8,128]{1,0:T(8,128)S(1)}, f32[8,128]{1,0:T(8,128)S(1)}, u32[]{:S(2)}, u32[]{:S(2)}) collective-permute-start(f32[8,128]{1,0:T(8,128)S(1)} %broadcast_select_fusion), channel_id=1, source_target_pairs={{0,4},{2,6},{4,0},{6,2},{8,12},{10,14},{12,8},{14,10},{16,20},{18,... | collective-permute-start | bytes 12296 | tf_op jit(solution)/shard_map/ppermute | solution.py:202
  8.6 7.4 %collective-permute-start.4 = (f32[8,128]{1,0:T(8,128)S(1)}, f32[8,128]{1,0:T(8,128)S(1)}, u32[]{:S(2)}, u32[]{:S(2)}) collective-permute-start(f32[8,128]{1,0:T(8,128)S(1)} %broadcast_select_fusion), channel_id=1, source_target_pairs={{0,6},{2,4},{4,2},{6,0},{8,14},{10,12},{12,10},{14,8},{16,22},{18,... | collective-permute-start | bytes 12296 | tf_op jit(solution)/shard_map/ppermute | solution.py:202
  10.8 12.2 %all-to-all-start = ((bf16[4,144,256]{2,1,0:T(8,128)(2,1)}), bf16[4,144,256]{2,1,0:T(8,128)(2,1)S(1)}, u32[]{:S(2)}, u32[]{:S(2)}) async-start(bf16[4,144,256]{2,1,0:T(8,128)(2,1)} %bitcast.23), calls=%async_computation | async-start | bytes 589824 | tf_op jit(solution)/shard_map/all_to_all | solution.py:203
  23.6 26.0 %all-to-all-start.1 = ((f32[12,8,128]{2,1,0:T(8,128)}), f32[12,8,128]{2,1,0:T(8,128)S(1)}, u32[]{:S(2)}, u32[]{:S(2)}) async-start(f32[12,8,128]{2,1,0:T(8,128)} %broadcast_in_dim.20), calls=%async_computation.1 | async-start | bytes 98304 | tf_op jit(solution)/shard_map/all_to_all | solution.py:207
  38.8 23.0 %collective-permute-start = (bf16[4,144,256]{2,1,0:T(8,128)(2,1)S(1)}, bf16[4,144,256]{2,1,0:T(8,128)(2,1)S(1)}, u32[]{:S(2)}, u32[]{:S(2)}) collective-permute-start(bf16[4,144,256]{2,1,0:T(8,128)(2,1)S(1)} %all-to-all-done.own_ref), channel_id=1, source_target_pairs={{0,8},{2,10},{4,12},{6,14},{8,16},{10,18},{12,20},{14,22},{16,24},... | collective-permute-start | bytes 884744 | tf_op jit(solution)/shard_map/ppermute | solution.py:215
  42.7 19.1 %collective-permute-start.1 = (bf16[4,144,256]{2,1,0:T(8,128)(2,1)S(1)}, bf16[4,144,256]{2,1,0:T(8,128)(2,1)S(1)}, u32[]{:S(2)}, u32[]{:S(2)}) collective-permute-start(bf16[4,144,256]{2,1,0:T(8,128)(2,1)S(1)} %all-to-all-done.own_ref), channel_id=1, source_target_pairs={{8,0},{10,2},{12,4},{14,6},{16,8},{18,10},{20,12},{22,14},{24,16},... | collective-permute-start | bytes 884744 | tf_op jit(solution)/shard_map/ppermute | solution.py:216
  49.6 0.9 %copy-start.1 = (s32[4,12288]{1,0:T(4,128)S(1)}, s32[4,12288]{1,0:T(4,128)}, u32[]{:S(2)}) copy-start(s32[4,12288]{1,0:T(4,128)} %index_ref.3) | copy-start | bytes 589828
  50.6 0.9 %copy-start.3 = (f32[4,12288]{1,0:T(4,128)S(1)}, f32[4,12288]{1,0:T(4,128)}, u32[]{:S(2)}) copy-start(f32[4,12288]{1,0:T(4,128)} %weight_ref.3) | copy-start | bytes 589828
  51.5 0.8 copy-start.5
  52.8 9.0 %collective-permute-start.5 = (f32[16,256]{1,0:T(8,128)S(1)}, f32[16,256]{1,0:T(8,128)S(1)}, u32[]{:S(2)}, u32[]{:S(2)}) collective-permute-start(f32[16,256]{1,0:T(8,128)S(1)} %interpolate.2.fown_ref), channel_id=1, source_target_pairs={{88,96},{90,98},{92,100},{94,102},{184,192},{186,194},{188,196},{1... | collective-permute-start | bytes 49160 | tf_op jit(solution)/shard_map/ppermute | solution.py:220
  67.0 14.2 %all-to-all-start.2 = ((bf16[8,144,256]{2,1,0:T(8,128)(2,1)}), bf16[8,144,256]{2,1,0:T(8,128)(2,1)S(1)}, u32[]{:S(2)}, u32[]{:S(2)}) async-start(bf16[8,144,256]{2,1,0:T(8,128)(2,1)} %propagate.1), calls=%async_computation.2 | async-start | bytes 1179648 | tf_op jit(solution)/shard_map/all_to_all | solution.py:232

commit v3 on v2

--- a/solution.py
+++ b/solution.py
@@ -1,3 +1,4 @@
+import functools
 import math
 
 import jax
@@ -14,6 +15,7 @@
 SUBSTEPS = 4
 OCEAN_ROWS = 8
 OCEAN_COLS = 192
+EXTRA = 16
 ROWS = 4
 
 courant = 0.45
@@ -45,81 +47,172 @@
     return jnp.concatenate([eastward, northward], 0).astype(jnp.bfloat16)
 
 
-def interpolate_body(
-    place_ref, gathered_ref, index_ref, weight_ref, mask_ref, out_ref
-):
+def pack_body(place_ref, spectrum_ref, currents_ref, out_ref, done):
+    members, bins, _ = spectrum_ref.shape
+    copy = pltpu.make_async_copy(spectrum_ref, out_ref.at[:, pl.ds(0, bins), :], done)
+    copy.start()
+    lane = lax.broadcasted_iota(jnp.int32, (OCEAN_ROWS, 128), 1)
+    ours = jnp.zeros((OCEAN_ROWS, 128), jnp.float32)
+    for c in range(2):
+        for i in range(4):
+            column = jnp.broadcast_to(currents_ref[c, :, i : i + 1], (OCEAN_ROWS, 128))
+            ours = jnp.where((lane & 7) == 4 * c + i, column, ours)
+    ours = jnp.where((lane >> 3) == place_ref[0], ours, 0.0)
+    high = ours.astype(jnp.bfloat16).astype(jnp.float32)
+    rest = ours - high
+    middle = rest.astype(jnp.bfloat16).astype(jnp.float32)
+    low = rest - middle
+    block = jnp.concatenate(
+        [jnp.concatenate([high, middle], 1), jnp.concatenate([low, jnp.zeros_like(low)], 1)], 0
+    ).astype(jnp.bfloat16)
+    for member in range(members):
+        out_ref[member, bins:, :] = block
+    copy.wait()
+
+
+def pack(place, spectrum, currents):
+    members, bins, cols = spectrum.shape
+    return pl.pallas_call(
+        pack_body,
+        out_shape=jax.ShapeDtypeStruct((members, bins + EXTRA, cols), jnp.bfloat16),
+        in_specs=[
+            pl.BlockSpec(memory_space=pltpu.SMEM),
+            pl.BlockSpec(memory_space=pl.ANY),
+            pl.BlockSpec(memory_space=pltpu.VMEM),
+        ],
+        out_specs=pl.BlockSpec(memory_space=pltpu.VMEM),
+        scratch_shapes=[pltpu.SemaphoreType.DMA],
+        compiler_params=pltpu.CompilerParams(vmem_limit_bytes=4 << 20),
+        cost_estimate=pl.CostEstimate(flops=100_000, bytes_accessed=700_000, transcendentals=0),
+        name="pack",
+    )(place, spectrum, currents)
+
+
+def unpack_body(own_ref, out_ref):
+    members = own_ref.shape[0]
+    table = jnp.zeros((OCEAN_ROWS, 128), jnp.float32)
+    for member in range(members):
+        block = own_ref[member].astype(jnp.float32)
+        upper, lower = block[:OCEAN_ROWS], block[OCEAN_ROWS:]
+        table += (upper[:, :128] + upper[:, 128:]) + lower[:, :128]
+    for group in range(out_ref.shape[0]):
+        out_ref[group] = table
+
+
+def unpack(own, groups):
+    members, depth, cols = own.shape
+    return pl.pallas_call(
+        unpack_body,
+        grid=(1,),
+        out_shape=jax.ShapeDtypeStruct((groups, OCEAN_ROWS, 128), jnp.float32),
+        in_specs=[pl.BlockSpec((members, EXTRA, cols), lambda i: (0, depth // EXTRA - 1, 0))],
+        out_specs=pl.BlockSpec((groups, OCEAN_ROWS, 128), lambda i: (0, 0, 0)),
+        compiler_params=pltpu.CompilerParams(vmem_limit_bytes=4 << 20),
+        cost_estimate=pl.CostEstimate(flops=20_000, bytes_accessed=100_000, transcendentals=0),
+        name="unpack",
+    )(own)
+
+
+def fetch_body(place_ref, index_ref, weight_ref, mask_ref, code_ref, share_ref, wet_ref):
+    cells = index_ref[...]
+    row_of = (cells * 5462) >> 20
+    column_of = cells - row_of * OCEAN_COLS
+    lane_of = ((column_of & 63) >> 2) * 8 + (column_of & 3)
+    code_ref[0] = row_of * 1024 + (column_of >> 6) * 128 + lane_of
+    share_ref[0] = weight_ref[...]
+    upper = place_ref[pl.program_id(0)] % 2 == 1
+    mask = jnp.where(upper, mask_ref[ROWS:, :], mask_ref[:ROWS, :])
+    wet_ref[0] = mask.astype(jnp.float32)
+
+
+def fetch(places, remap_index, remap_weights, wet_mask):
+    count = places.shape[0]
+    cols = wet_mask.shape[1]
+    block = ROWS * cols
+    return pl.pallas_call(
+        fetch_body,
+        grid_spec=pltpu.PrefetchScalarGridSpec(
+            num_scalar_prefetch=1,
+            grid=(count,),
+            in_specs=[
+                pl.BlockSpec((4, block), lambda i, place: (0, place[i])),
+                pl.BlockSpec((4, block), lambda i, place: (0, place[i])),
+                pl.BlockSpec((2 * ROWS, cols), lambda i, place: (place[i] // 2, 0)),
+            ],
+            out_specs=[
+                pl.BlockSpec((1, 4, block), lambda i, place: (i, 0, 0)),
+                pl.BlockSpec((1, 4, block), lambda i, place: (i, 0, 0)),
+                pl.BlockSpec((1, ROWS, cols), lambda i, place: (i, 0, 0)),
+            ],
+        ),
+        out_shape=[
+            jax.ShapeDtypeStruct((count, 4, block), jnp.int32),
+            jax.ShapeDtypeStruct((count, 4, block), jnp.float32),
+            jax.ShapeDtypeStruct((count, ROWS, cols), jnp.float32),
+        ],
+        compiler_params=pltpu.CompilerParams(vmem_limit_bytes=4 << 20),
+        cost_estimate=pl.CostEstimate(flops=100_000, bytes_accessed=300_000, transcendentals=0),
+        name="fetch",
+    )(places, remap_index, remap_weights, wet_mask)
+
+
+def interpolate_body(blocks, gathered_ref, code_ref, share_ref, wet_ref, out_ref):
     groups = gathered_ref.shape[0]
-    cols = mask_ref.shape[1]
-    rows = ROWS
+    rows, cols = wet_ref.shape[1:]
     row_ids = lax.broadcasted_iota(jnp.int32, (OCEAN_ROWS, 128), 0)
     tables = []
     for part in range(groups // 4):
         pieces = [gathered_ref[4 * part + i] for i in range(4)]
         tables.append((pieces[0] + pieces[1]) + (pieces[2] + pieces[3]))
-    for chunk in range(rows * cols // 128):
-        lanes = slice(chunk * 128, chunk * 128 + 128)
-        cells = index_ref[:, lanes]
-        shares = weight_ref[:, lanes]
-        row_of = (cells * 5462) >> 20
-        column_of = cells - row_of * OCEAN_COLS
-        lane_of = ((column_of & 63) >> 2) * 8 + (column_of & 3)
-        part_of = column_of >> 6
-        totals = [jnp.zeros((OCEAN_ROWS, 128), jnp.float32) for _ in range(2)]
-        for corner in range(4):
-            row_b = jnp.broadcast_to(row_of[corner : corner + 1], (OCEAN_ROWS, 128))
-            lane_b = jnp.broadcast_to(lane_of[corner : corner + 1], (OCEAN_ROWS, 128))
-            part_b = jnp.broadcast_to(part_of[corner : corner + 1], (OCEAN_ROWS, 128))
-            share_b = jnp.broadcast_to(shares[corner : corner + 1], (OCEAN_ROWS, 128))
-            weight = jnp.where(row_b == row_ids, share_b, 0.0)
+    for place, block in enumerate(blocks):
+        base = place * 4 * rows
+        for chunk in range(rows * cols // 128):
+            lanes = slice(chunk * 128, chunk * 128 + 128)
+            codes = code_ref[block, :, lanes]
+            shares = share_ref[block, :, lanes]
+            totals = [jnp.zeros((OCEAN_ROWS, 128), jnp.float32) for _ in range(2)]
+            for corner in range(4):
+                code_b = jnp.broadcast_to(codes[corner : corner + 1], (OCEAN_ROWS, 128))
+                share_b = jnp.broadcast_to(shares[corner : corner + 1], (OCEAN_ROWS, 128))
+                part_b = (code_b >> 7) & 7
+                weight = jnp.where((code_b >> 10) == row_ids, share_b, 0.0)
+                for c in range(2):
+                    lane_b = (code_b & 127) + 4 * c
+                    picked = jnp.take_along_axis(tables[0], lane_b, axis=1)
+                    for part in range(1, len(tables)):
+                        other = jnp.take_along_axis(tables[part], lane_b, axis=1)
+                        picked = jnp.where(part_b == part, other, picked)
+                    totals[c] += picked * weight
+            row = chunk * 128 // cols
+            spot = slice(chunk * 128 % cols, chunk * 128 % cols + 128)
             for c in range(2):
-                picked = jnp.take_along_axis(tables[0], lane_b + 4 * c, axis=1)
-                for part in range(1, len(tables)):
-                    other = jnp.take_along_axis(tables[part], lane_b + 4 * c, axis=1)
-                    picked = jnp.where(part_b == part, other, picked)
-                totals[c] += picked * weight
-        row = chunk * 128 // cols
-        spot = slice(chunk * 128 % cols, chunk * 128 % cols + 128)
-        for c in range(2):
-            out_ref[c * rows + row : c * rows + row + 1, spot] = courant * jnp.sum(
-                totals[c], axis=0, keepdims=True
-            )
-    upper = place_ref[pl.program_id(0)] % 2 == 1
-    mask = jnp.where(upper, mask_ref[rows : 2 * rows, :], mask_ref[0:rows, :])
-    out_ref[2 * rows : 3 * rows, :] = mask.astype(jnp.float32)
-    out_ref[3 * rows :, :] = jnp.zeros((rows, cols), jnp.float32)
-
-
-def interpolate(places, gathered, remap_index, remap_weights, wet_mask):
-    count = places.shape[0]
-    cols = wet_mask.shape[1]
-    block = ROWS * cols
-    return pl.pallas_call(
-        interpolate_body,
-        grid_spec=pltpu.PrefetchScalarGridSpec(
-            num_scalar_prefetch=1,
-            grid=(count,),
-            in_specs=[
-                pl.BlockSpec(gathered.shape, lambda i, place: (0, 0, 0)),
-                pl.BlockSpec((4, block), lambda i, place: (0, place[i])),
-                pl.BlockSpec((4, block), lambda i, place: (0, place[i])),
-                pl.BlockSpec((2 * ROWS, cols), lambda i, place: (place[i] // 2, 0)),
-            ],
-            out_specs=pl.BlockSpec((4 * ROWS, cols), lambda i, place: (i, 0)),
-        ),
-        out_shape=jax.ShapeDtypeStruct((count * 4 * ROWS, cols), jnp.float32),
+                at = base + c * rows + row
+                out_ref[at : at + 1, spot] = courant * jnp.sum(totals[c], axis=0, keepdims=True)
+        out_ref[base + 2 * rows : base + 3 * rows, :] = wet_ref[block]
+        out_ref[base + 3 * rows : base + 4 * rows, :] = jnp.zeros((rows, cols), jnp.float32)
+
+
+def interpolate(blocks, gathered, codes, shares, wet):
+    count = len(blocks)
+    rows, cols = wet.shape[1:]
+    return pl.pallas_call(
+        functools.partial(interpolate_body, blocks),
+        out_shape=jax.ShapeDtypeStruct((count * 4 * rows, cols), jnp.float32),
+        in_specs=[pl.BlockSpec(memory_space=pltpu.VMEM)] * 4,
+        out_specs=pl.BlockSpec(memory_space=pltpu.VMEM),
         compiler_params=pltpu.CompilerParams(vmem_limit_bytes=4 << 20),
         cost_estimate=pl.CostEstimate(
             flops=2_000_000 * count, bytes_accessed=100_000 * count, transcendentals=0
         ),
         name="interpolate",
-    )(places, gathered, remap_index, remap_weights, wet_mask)
+    )(gathered, codes, shares, wet)
 
 
 def propagate_body(
     edge_ref, below_ref, own_ref, above_ref, fown_ref, fbeside_ref, fother_ref, east_ref, north_ref,
     out_ref, fbelow_ref, fabove_ref,
 ):
-    rows, bins, cols = own_ref.shape
+    rows, bins, cols = below_ref.shape
     tile = 16
     deep = 4 * rows
     fother = fother_ref[...]
@@ -166,7 +259,7 @@
 
 
 def propagate(edges, below, own, above, fown, fbeside, fother, east, north):
-    rows, bins, cols = own.shape
+    rows, bins, cols = below.shape
     return pl.pallas_call(
         propagate_body,
         out_shape=jax.ShapeDtypeStruct((2 * rows, bins, cols), jnp.bfloat16),
@@ -178,6 +271,52 @@
         cost_estimate=pl.CostEstimate(flops=40_000_000, bytes_accessed=1_600_000, transcendentals=0),
         name="propagate",
     )(edges, below, own, above, fown, fbeside, fother, east, north)
+
+
+def finish_body(comp_ref, fragment_ref, source_ref, kernel_ref, wet_ref, updated_ref, stokes_ref):
+    rows = updated_ref.shape[0]
+    steps = pl.num_programs(0)
+    fragment = fragment_ref[...]
+    source = jnp.dot(source_ref[...], fragment, preferred_element_type=jnp.float32)
+    first = (comp_ref[0] * steps + pl.program_id(0)) * rows
+    returned = fragment_ref[pl.ds(pl.multiple_of(first, 16), rows), :].astype(jnp.float32)
+    updated_ref[...] = (wet_ref[...] * jnp.maximum(returned + source, 0.0)).astype(jnp.bfloat16)
+
+    @pl.when(pl.program_id(0) == 0)
+    def _():
+        stokes_ref[...] = jnp.dot(kernel_ref[...], fragment, preferred_element_type=jnp.float32)
+
+
+def finish(comp_index, fragment, source_matrix, kernel, wet_points):
+    bins, points = fragment.shape
+    local_bins = source_matrix.shape[0]
+    levels = kernel.shape[0]
+    steps = 3
+    tile = local_bins // steps
+    return pl.pallas_call(
+        finish_body,
+        grid=(steps,),
+        out_shape=[
+            jax.ShapeDtypeStruct((local_bins, points), jnp.bfloat16),
+            jax.ShapeDtypeStruct((levels, points), jnp.float32),
+        ],
+        in_specs=[
+            pl.BlockSpec(memory_space=pltpu.SMEM),
+            pl.BlockSpec((bins, points), lambda i: (0, 0)),
+            pl.BlockSpec((tile, bins), lambda i: (i, 0)),
+            pl.BlockSpec((levels, bins), lambda i: (0, 0)),
+            pl.BlockSpec((1, points), lambda i: (0, 0)),
+        ],
+        out_specs=[
+            pl.BlockSpec((tile, points), lambda i: (i, 0)),
+            pl.BlockSpec((levels, points), lambda i: (0, 0)),
+        ],
+        compiler_params=pltpu.CompilerParams(vmem_limit_bytes=8 << 20),
+        cost_estimate=pl.CostEstimate(
+            flops=2 * bins * points * (local_bins + levels), bytes_accessed=2_500_000, transcendentals=0
+        ),
+        name="finish",
+    )(comp_index.reshape(1), fragment, source_matrix, kernel, wet_points)
 
 
 def step(spectrum, wet_mask, currents, remap_index, remap_weights, source_matrix):
@@ -193,33 +332,31 @@
     near = [[ROWS * g + i for i in range(ROWS)] for g in range(groups)]
     far = [[ROWS * g + i for g in range(groups)] for i in range(ROWS)]
 
-    lane = jnp.arange(128, dtype=jnp.int32)
-    ours = jnp.concatenate([currents[0], currents[1]], axis=1)
-    ours = jnp.where((lane // 8 == wide_index % 16)[None, :], jnp.tile(ours, (1, 16)), 0.0)
-    table = ours
-    for turn in range(1, ROWS):
-        swap = [(i, i - i % ROWS + (i % ROWS ^ turn)) for i in range(wides)]
-        table = table + lax.ppermute(ours, "wide", swap)
+    message = pack((wide_index % 16).reshape(1), spectrum.reshape(ROWS, share, points), currents)
     own = lax.all_to_all(
-        spectrum.reshape(ROWS, share, points),
-        "wide", split_axis=0, concat_axis=0, tiled=True, axis_index_groups=near,
-    )
+        message, "wide", split_axis=0, concat_axis=0, tiled=True, axis_index_groups=near
+    )
+    places = jnp.stack(
+        [jnp.maximum(group_index - 1, 0), group_index, jnp.minimum(group_index + 1, groups - 1)]
+    )
+    fetched = fetch(places, remap_index, remap_weights, wet_mask)
     table = lax.all_to_all(
-        jnp.broadcast_to(table[None], (groups, OCEAN_ROWS, 128)),
+        unpack(own, groups),
         "wide", split_axis=0, concat_axis=0, tiled=True, axis_index_groups=far,
     )
     total = strips * wides
     upward = [(i, i + ROWS) for i in range(total - ROWS)]
     downward = [(i + ROWS, i) for i in range(total - ROWS)]
     chain = ("strip", "wide")
-    below = lax.ppermute(own, chain, upward)
-    above = lax.ppermute(own, chain, downward)
-    args = (table, remap_index, remap_weights, wet_mask)
-    fown = interpolate(group_index.reshape(1), *args)
-    crossing = [(s * wides + wides - ROWS + i, (s + 1) * wides + i) for s in range(strips - 1) for i in range(ROWS)]
+    bins = own[:, :share]
+    below = lax.ppermute(bins, chain, upward)
+    above = lax.ppermute(bins, chain, downward)
+    fown = interpolate((1,), table, *fetched)
+    crossing = [
+        (s * wides + wides - ROWS + i, (s + 1) * wides + i) for s in range(strips - 1) for i in range(ROWS)
+    ]
     fother = lax.ppermute(fown, chain, crossing + [(b, a) for a, b in crossing])
-    beside = jnp.stack([jnp.maximum(group_index - 1, 0), jnp.minimum(group_index + 1, groups - 1)])
-    fbeside = interpolate(beside, *args)
+    fbeside = interpolate((0, 2), table, *fetched)
     edges = jnp.stack([group_index == 0, group_index == groups - 1]).astype(jnp.int32)
 
     first_bin = comp_index * local_bins + member * share
@@ -235,14 +372,9 @@
 
     level_rows = LEVELS // comps
     kernel = stokes_kernel(comps * local_bins, comp_index * level_rows, level_rows)
-    source_part = jnp.dot(source_matrix, fragment, preferred_element_type=jnp.float32)
-    drift_part = jnp.dot(kernel, fragment, preferred_element_type=jnp.float32)
-    returned = lax.dynamic_slice_in_dim(fragment, comp_index * local_bins, local_bins, 0)
     wet_points = lax.dynamic_slice_in_dim(wet_mask, wide_index, 1, 0).astype(jnp.float32)
-    updated = (
-        wet_points * jnp.maximum(returned.astype(jnp.float32) + source_part, 0.0)
-    ).astype(jnp.bfloat16)
-    return (updated, drift_part.reshape(2, level_rows, points))
+    updated, stokes = finish(comp_index, fragment, source_matrix, kernel, wet_points)
+    return (updated, stokes.reshape(2, level_rows, points))
 
 
 def solution(mesh):

time: 84 us -> 79.8 us (0.950)
  starting transfers between devices: 43.8 us -> 31.3 us
  waiting for transfers between devices: 23.8 us -> 33.5 us
  Pallas kernels: 7.17 us -> 10.7 us
  local copies, waits for them, and re-layouts: 4.44 us -> 1.92 us
  matrix products: 2.11 us -> 0 us
    all_to_all x2, starting transfers between devices: 19.5 us -> 8.92 us  [the longest x1 4.62 us: step(): lax.all_to_all(unpack(own, groups), 'wide', split_axis=0, concat_axis=0,...]
    all_to_all x2, waiting for transfers between devices: 8.54 us -> 17.4 us  [the longest x1 10.1 us: step(): lax.all_to_all(unpack(own, groups), 'wide', split_axis=0, concat_axis=0,...]
    pallas_call x2 -> x6, Pallas kernels: 2.06 us -> 5.61 us  [the longest x1 2.11 us: finish(): pl.pallas_call(finish_body, grid=(steps,), out_shape=[jax.ShapeDtypeStruc...]
    dot_general x2 -> x0, matrix products: 2.11 us -> none  [the longest x1 1.27 us: step(): jnp.dot(source_matrix, fragment, preferred_element_type=jnp.float32)]
    ppermute x5 -> x2, starting transfers between devices: 18.3 us -> 16.4 us  [the longest x1 12.1 us: step(): above = lax.ppermute(bins, chain, downward)]
    unnamed x14 -> x11, local copies, waits for them, and re-layouts: 2.68 us -> 1.75 us
  transfers between devices with their start and end apart: 9 -> 6, of which waited for: 4 -> 4; matrix products, arithmetic and copies ran while one was open for 1% -> 1% of each run, Pallas kernels for 2% -> 3%
where the time goes in v3:
time: 79.8 us; the launch traced here: 79.3 us
  waiting for transfers between devices  33.5 us (42%)
  starting transfers between devices  31.3 us (39%)
  Pallas kernels  10.7 us (13%)
  local copies, waits for them, and re-layouts  1.92 us (2%)
  other arithmetic  1.09 us (1%)
    ppermute x1, starting transfers between devices, step(): above = lax.ppermute(bins, chain, downward)  12.1 us
    all_to_all x1, waiting for transfers between devices, step(): lax.all_to_all(spread, ('wide', 'comp'), split_axis=0, concat_axis=0, til...  10.6 us
    all_to_all x1, waiting for transfers between devices, step(): lax.all_to_all(unpack(own, groups), 'wide', split_axis=0, concat_axis=0,...  10.1 us
    all_to_all x1, waiting for transfers between devices, step(): lax.all_to_all(message, 'wide', split_axis=0, concat_axis=0, tiled=True,...  7.38 us
    ppermute x1, waiting for transfers between devices, step(): fother = lax.ppermute(fown, chain, crossing + [(b, a) for a, b in crossing])  5.52 us
    pallas_call x1, Pallas kernels, propagate(): pl.pallas_call(propagate_body, out_shape=jax.ShapeDtypeStruct((2 * rows,...  5.09 us
    all_to_all x1, starting transfers between devices, step(): lax.all_to_all(unpack(own, groups), 'wide', split_axis=0, concat_axis=0,...  4.62 us
    all_to_all x1, starting transfers between devices, step(): lax.all_to_all(message, 'wide', split_axis=0, concat_axis=0, tiled=True,...  4.3 us
  transfers between devices with their start and end apart: 6, of which 4 were waited for; matrix products, arithmetic and copies ran while one was open for 1% of the time, Pallas kernels for 3%

profile of v3, /device:TPU:32, one launch (start us, length us, event | category | flops | bytes accessed | tf_op | source)
XLA Modules:
  0.0 79.3 jit_solution(3186366196660724303)
XLA Ops:
  0.6 0.8 copy.8.currents_ref
  1.4 0.0 copy-start.1
  1.4 1.0 %copy-done.1 = bf16[576,256]{1,0:T(8,128)(2,1)S(1)} copy-done((bf16[576,256]{1,0:T(8,128)(2,1)S(1)}, bf16[576,256]{1,0:T(8,128)(2,1)}, u32[]{:S(2)}) %copy-start.1) | copy-done | bytes 294936
  2.4 0.0 copy-start.2
  2.4 0.0 copy-start.3
  2.4 0.0 copy-start.4
  2.4 0.8 %pack.1 = bf16[4,160,256]{2,1,0:T(8,128)(2,1)} custom-call(s32[1]{0:T(128)} %bitcast.3.place_ref, bf16[4,144,256]{2,1,0:T(8,128)(2,1)S(1)} %bitcast.11, f32[2,8,4]{2,1,0:T(8,128)S(1)} %copy.8.currents_ref), custom_call_target="tpu_custom_call" | custom-call | flops 100000 | bytes 700000 | tf_op jit(solution)/shard_map/pack/pallas_call | solution.py:75
  3.2 4.3 %all-to-all-start = ((bf16[4,160,256]{2,1,0:T(8,128)(2,1)}), bf16[4,160,256]{2,1,0:T(8,128)(2,1)S(1)}, u32[]{:S(2)}, u32[]{:S(2)}) async-start(bf16[4,160,256]{2,1,0:T(8,128)(2,1)} %pack.1), calls=%async_computation | async-start | bytes 655360 | tf_op jit(solution)/shard_map/all_to_all | solution.py:336
  7.5 0.7 dynamic-slice_convert_fusion.wet_ref
  8.2 0.1 sine_multiply_fusion
  8.3 0.1 fusion.13
  8.4 7.4 %all-to-all-done.own_ref = bf16[4,160,256]{2,1,0:T(8,128)(2,1)S(1)} async-done(((bf16[4,160,256]{2,1,0:T(8,128)(2,1)}), bf16[4,160,256]{2,1,0:T(8,128)(2,1)S(1)}, u32[]{:S(2)}, u32[]{:S(2)}) %all-to-all-start) | async-done | bytes 327712 | tf_op jit(solution)/shard_map/all_to_all | solution.py:336
  15.8 4.3 %collective-permute-start = (bf16[4,144,256]{2,1,0:T(8,128)(2,1)S(1)}, bf16[4,144,256]{2,1,0:T(8,128)(2,1)S(1)}, u32[]{:S(2)}, u32[]{:S(2)}) collective-permute-start(bf16[4,144,256]{2,1,0:T(8,128)(2,1)S(1)} %slice.4), channel_id=1, source_target_pairs={{0,8},{2,10},{4,12},{6,14},{8,16},{10,18},{12,20},{14,22},{16,24},... | collective-permute-start | bytes 884744 | tf_op jit(solution)/shard_map/ppermute | solution.py:352
  20.1 12.1 %collective-permute-start.1 = (bf16[4,144,256]{2,1,0:T(8,128)(2,1)S(1)}, bf16[4,144,256]{2,1,0:T(8,128)(2,1)S(1)}, u32[]{:S(2)}, u32[]{:S(2)}) collective-permute-start(bf16[4,144,256]{2,1,0:T(8,128)(2,1)S(1)} %slice.4), channel_id=1, source_target_pairs={{8,0},{10,2},{12,4},{14,6},{16,8},{18,10},{20,12},{22,14},{24,16},... | collective-permute-start | bytes 884744 | tf_op jit(solution)/shard_map/ppermute | solution.py:353
  32.2 0.6 unpack.1
  32.8 4.6 %all-to-all-start.1 = ((f32[12,8,128]{2,1,0:T(8,128)}), f32[12,8,128]{2,1,0:T(8,128)S(1)}, u32[]{:S(2)}, u32[]{:S(2)}) async-start(f32[12,8,128]{2,1,0:T(8,128)} %unpack.1), calls=%async_computation.1 | async-start | bytes 98304 | tf_op jit(solution)/shard_map/all_to_all | solution.py:343
  37.4 0.1 pad_add_fusion.place_ref
  37.5 0.0 copy-done.2
  37.5 0.0 copy-done.3
  37.5 0.0 copy-done.4
  37.5 0.7 fetch.1
  38.2 10.1 %all-to-all-done.1.gathered_ref = f32[12,8,128]{2,1,0:T(8,128)S(1)} async-done(((f32[12,8,128]{2,1,0:T(8,128)}), f32[12,8,128]{2,1,0:T(8,128)S(1)}, u32[]{:S(2)}, u32[]{:S(2)}) %all-to-all-start.1) | async-done | bytes 49184 | tf_op jit(solution)/shard_map/all_to_all | solution.py:343
  48.3 0.5 interpolate.2.fown_ref
  48.8 2.5 %collective-permute-start.2 = (f32[16,256]{1,0:T(8,128)S(1)}, f32[16,256]{1,0:T(8,128)S(1)}, u32[]{:S(2)}, u32[]{:S(2)}) collective-permute-start(f32[16,256]{1,0:T(8,128)S(1)} %interpolate.2.fown_ref), channel_id=1, source_target_pairs={{88,96},{90,98},{92,100},{94,102},{184,192},{186,194},{188,196},{1... | collective-permute-start | bytes 49160 | tf_op jit(solution)/shard_map/ppermute | solution.py:358
  51.2 0.1 add_convert_fusion.edge_ref
  51.3 0.9 %interpolate.3.fbeside_ref = f32[32,256]{1,0:T(8,128)S(1)} custom-call(f32[12,8,128]{2,1,0:T(8,128)S(1)} %all-to-all-done.1.gathered_ref, s32[3,4,1024]{2,1,0:T(4,128)S(1)} %get-tuple-element.7.code_ref, f32[3,4,1024]{2,1,0:T(4,128)S(1)} %get-tuple-element.8.share_ref, f32[3,4,256]{2,1,0:T(4,128)S(1)} %get-tuple-element.9.wet_ref), custom_call_target="tpu_custom_call" | custom-call | flops 4000000 | bytes 200000 | tf_op jit(solution)/shard_map/interpolate/pallas_call | solution.py:198
  52.2 5.5 %collective-permute-done.2.fother_ref = f32[16,256]{1,0:T(8,128)S(1)} collective-permute-done((f32[16,256]{1,0:T(8,128)S(1)}, f32[16,256]{1,0:T(8,128)S(1)}, u32[]{:S(2)}, u32[]{:S(2)}) %collective-permute-start.2) | collective-permute-done | bytes 16416 | tf_op jit(solution)/shard_map/ppermute | solution.py:358
  57.7 0.0 collective-permute-done.below_ref
  57.7 0.0 collective-permute-done.1.above_ref
  57.7 0.1 broadcast_in_dim.4.east_ref
  57.8 0.1 broadcast_in_dim.5.north_ref
  57.9 0.0 copy-start
  57.9 5.1 %propagate.1 = bf16[8,144,256]{2,1,0:T(8,128)(2,1)} custom-call(s32[2]{0:T(128)S(1)} %add_convert_fusion.edge_ref, bf16[4,144,256]{2,1,0:T(8,128)(2,1)S(1)} %collective-permute-done.below_ref, bf16[4,160,256]{2,1,0:T(8,128)(2,1)S(1)} %all-to-all-done.own_ref, bf16[4,144,256]{2,1,0:T(8,128)(2,1)S(1)} %collective-permute-done.1.above_ref, ...), custom_call_target="tpu_custom_call" | custom-call | flops 40000000 | bytes 1600000 | tf_op jit(solution)/shard_map/propagate/pallas_call | solution.py:263
  63.0 3.5 %all-to-all-start.2 = ((bf16[8,144,256]{2,1,0:T(8,128)(2,1)}), bf16[8,144,256]{2,1,0:T(8,128)(2,1)S(1)}, u32[]{:S(2)}, u32[]{:S(2)}) async-start(bf16[8,144,256]{2,1,0:T(8,128)(2,1)} %propagate.1), calls=%async_computation.2 | async-start | bytes 1179648 | tf_op jit(solution)/shard_map/all_to_all | solution.py:369
  66.5 0.1 multiply_convert_fusion.1
  66.6 10.6 %all-to-all-done.2 = bf16[8,144,256]{2,1,0:T(8,128)(2,1)S(1)} async-done(((bf16[8,144,256]{2,1,0:T(8,128)(2,1)}), bf16[8,144,256]{2,1,0:T(8,128)(2,1)S(1)}, u32[]{:S(2)}, u32[]{:S(2)}) %all-to-all-start.2) | async-done | bytes 589856 | tf_op jit(solution)/shard_map/all_to_all | solution.py:369
  77.2 0.0 copy-done
  77.2 2.1 %finish.1 = (bf16[576,256]{1,0:T(8,128)(2,1)}, f32[32,256]{1,0:T(8,128)}) custom-call(s32[1]{0:T(128)} %bitcast.comp_ref, bf16[1152,256]{1,0:T(8,128)(2,1)S(1)} %bitcast.10, bf16[576,1152]{1,0:T(8,128)(2,1)S(1)} %copy-done, bf16[32,1152]{1,0:T(8,128)(2,1)S(1)} %pad_maximum_fusion.kernel_ref, f32[1,256]{1,0:T(1,128)S(1)} %dynamic-slice_convert_fusion.wet_ref), custom_call_target="tpu_custom_call" | custom-call | flops 358612992 | bytes 2500000 | tf_op jit(solution)/shard_map/finish/pallas_call | solution.py:296
  (4 shorter events, 0.0 us)
Async XLA Ops:
  1.4 1.0 %copy-start.1 = (bf16[576,256]{1,0:T(8,128)(2,1)S(1)}, bf16[576,256]{1,0:T(8,128)(2,1)}, u32[]{:S(2)}) copy-start(bf16[576,256]{1,0:T(8,128)(2,1)} %param.6) | copy-start | bytes 884740
  2.4 35.1 %copy-start.2 = (s32[4,12288]{1,0:T(4,128)S(1)}, s32[4,12288]{1,0:T(4,128)}, u32[]{:S(2)}) copy-start(s32[4,12288]{1,0:T(4,128)} %index_ref.1) | copy-start | bytes 589828
  2.4 35.1 %copy-start.3 = (f32[4,12288]{1,0:T(4,128)S(1)}, f32[4,12288]{1,0:T(4,128)}, u32[]{:S(2)}) copy-start(f32[4,12288]{1,0:T(4,128)} %weight_ref.1) | copy-start | bytes 589828
  2.4 35.1 %copy-start.4 = (s32[48,256]{1,0:T(8,128)S(1)}, s32[48,256]{1,0:T(8,128)}, u32[]{:S(2)}) copy-start(s32[48,256]{1,0:T(8,128)} %mask_ref.1) | copy-start | bytes 147460
  3.2 12.5 %all-to-all-start = ((bf16[4,160,256]{2,1,0:T(8,128)(2,1)}), bf16[4,160,256]{2,1,0:T(8,128)(2,1)S(1)}, u32[]{:S(2)}, u32[]{:S(2)}) async-start(bf16[4,160,256]{2,1,0:T(8,128)(2,1)} %pack.1), calls=%async_computation | async-start | bytes 655360 | tf_op jit(solution)/shard_map/all_to_all | solution.py:336
  15.8 41.9 %collective-permute-start = (bf16[4,144,256]{2,1,0:T(8,128)(2,1)S(1)}, bf16[4,144,256]{2,1,0:T(8,128)(2,1)S(1)}, u32[]{:S(2)}, u32[]{:S(2)}) collective-permute-start(bf16[4,144,256]{2,1,0:T(8,128)(2,1)S(1)} %slice.4), channel_id=1, source_target_pairs={{0,8},{2,10},{4,12},{6,14},{8,16},{10,18},{12,20},{14,22},{16,24},... | collective-permute-start | bytes 884744 | tf_op jit(solution)/shard_map/ppermute | solution.py:352
  20.1 37.7 %collective-permute-start.1 = (bf16[4,144,256]{2,1,0:T(8,128)(2,1)S(1)}, bf16[4,144,256]{2,1,0:T(8,128)(2,1)S(1)}, u32[]{:S(2)}, u32[]{:S(2)}) collective-permute-start(bf16[4,144,256]{2,1,0:T(8,128)(2,1)S(1)} %slice.4), channel_id=1, source_target_pairs={{8,0},{10,2},{12,4},{14,6},{16,8},{18,10},{20,12},{22,14},{24,16},... | collective-permute-start | bytes 884744 | tf_op jit(solution)/shard_map/ppermute | solution.py:353
  32.8 15.5 %all-to-all-start.1 = ((f32[12,8,128]{2,1,0:T(8,128)}), f32[12,8,128]{2,1,0:T(8,128)S(1)}, u32[]{:S(2)}, u32[]{:S(2)}) async-start(f32[12,8,128]{2,1,0:T(8,128)} %unpack.1), calls=%async_computation.1 | async-start | bytes 98304 | tf_op jit(solution)/shard_map/all_to_all | solution.py:343
  48.8 9.0 %collective-permute-start.2 = (f32[16,256]{1,0:T(8,128)S(1)}, f32[16,256]{1,0:T(8,128)S(1)}, u32[]{:S(2)}, u32[]{:S(2)}) collective-permute-start(f32[16,256]{1,0:T(8,128)S(1)} %interpolate.2.fown_ref), channel_id=1, source_target_pairs={{88,96},{90,98},{92,100},{94,102},{184,192},{186,194},{188,196},{1... | collective-permute-start | bytes 49160 | tf_op jit(solution)/shard_map/ppermute | solution.py:358
  57.9 19.3 %copy-start = (bf16[576,1152]{1,0:T(8,128)(2,1)S(1)}, bf16[576,1152]{1,0:T(8,128)(2,1)}, u32[]{:S(2)}) copy-start(bf16[576,1152]{1,0:T(8,128)(2,1)} %source_ref.1) | copy-start | bytes 3981316
  63.0 14.2 %all-to-all-start.2 = ((bf16[8,144,256]{2,1,0:T(8,128)(2,1)}), bf16[8,144,256]{2,1,0:T(8,128)(2,1)S(1)}, u32[]{:S(2)}, u32[]{:S(2)}) async-start(bf16[8,144,256]{2,1,0:T(8,128)(2,1)} %propagate.1), calls=%async_computation.2 | async-start | bytes 1179648 | tf_op jit(solution)/shard_map/all_to_all | solution.py:369

commit v4 on v3

--- a/solution.py
+++ b/solution.py
@@ -47,15 +47,22 @@
     return jnp.concatenate([eastward, northward], 0).astype(jnp.bfloat16)
 
 
-def pack_body(place_ref, spectrum_ref, currents_ref, out_ref, done):
+def pack_body(place_ref, spectrum_ref, currents_ref, out_ref, local_ref, done):
     members, bins, _ = spectrum_ref.shape
-    copy = pltpu.make_async_copy(spectrum_ref, out_ref.at[:, pl.ds(0, bins), :], done)
+    fetch_currents = pltpu.make_async_copy(currents_ref, local_ref, done.at[1])
+    fetch_currents.start()
+    copy = pltpu.make_async_copy(spectrum_ref, out_ref.at[:, pl.ds(0, bins), :], done.at[0])
     copy.start()
     lane = lax.broadcasted_iota(jnp.int32, (OCEAN_ROWS, 128), 1)
+    diagonal = lax.broadcasted_iota(jnp.int32, (OCEAN_ROWS, OCEAN_ROWS), 0) == lax.broadcasted_iota(
+        jnp.int32, (OCEAN_ROWS, OCEAN_ROWS), 1
+    )
+    fetch_currents.wait()
     ours = jnp.zeros((OCEAN_ROWS, 128), jnp.float32)
     for c in range(2):
         for i in range(4):
-            column = jnp.broadcast_to(currents_ref[c, :, i : i + 1], (OCEAN_ROWS, 128))
+            line = jnp.broadcast_to(local_ref[c, i : i + 1, :], (OCEAN_ROWS, OCEAN_ROWS))
+            column = jnp.sum(jnp.where(diagonal, line, 0.0), axis=1, keepdims=True)
             ours = jnp.where((lane & 7) == 4 * c + i, column, ours)
     ours = jnp.where((lane >> 3) == place_ref[0], ours, 0.0)
     high = ours.astype(jnp.bfloat16).astype(jnp.float32)
@@ -77,15 +84,17 @@
         out_shape=jax.ShapeDtypeStruct((members, bins + EXTRA, cols), jnp.bfloat16),
         in_specs=[
             pl.BlockSpec(memory_space=pltpu.SMEM),
-            pl.BlockSpec(memory_space=pl.ANY),
-            pl.BlockSpec(memory_space=pltpu.VMEM),
+            pl.BlockSpec(memory_space=pltpu.HBM),
+            pl.BlockSpec(memory_space=pltpu.HBM),
         ],
         out_specs=pl.BlockSpec(memory_space=pltpu.VMEM),
-        scratch_shapes=[pltpu.SemaphoreType.DMA],
-        compiler_params=pltpu.CompilerParams(vmem_limit_bytes=4 << 20),
+        scratch_shapes=[
+            pltpu.VMEM((2, 4, OCEAN_ROWS), jnp.float32),
+            pltpu.SemaphoreType.DMA((2,)),
+        ],
         cost_estimate=pl.CostEstimate(flops=100_000, bytes_accessed=700_000, transcendentals=0),
         name="pack",
-    )(place, spectrum, currents)
+    )(place, spectrum, jnp.transpose(currents, (0, 2, 1)))
 
 
 def unpack_body(own_ref, out_ref):
@@ -209,10 +218,11 @@
 
 
 def propagate_body(
-    edge_ref, below_ref, own_ref, above_ref, fown_ref, fbeside_ref, fother_ref, east_ref, north_ref,
+    edge_ref, first_ref, own_ref, second_ref, fown_ref, fbeside_ref, fother_ref, east_ref, north_ref,
     out_ref, fbelow_ref, fabove_ref,
 ):
-    rows, bins, cols = below_ref.shape
+    rows, bins, cols = first_ref.shape
+    swapped = edge_ref[2] == 1
     tile = 16
     deep = 4 * rows
     fother = fother_ref[...]
@@ -225,8 +235,14 @@
         speed_north = jnp.concatenate([north_ref[spot, :]] * (cols // 128), 1)
         energy, masks = [], []
         coefs = []
-        for source, fields in ((below_ref, fbelow_ref), (own_ref, fown_ref), (above_ref, fabove_ref)):
+        for side, fields in enumerate((fbelow_ref, fown_ref, fabove_ref)):
             for row in range(rows):
+                if side == 1:
+                    cells = own_ref[row, spot, :].astype(jnp.float32)
+                else:
+                    first = first_ref[row, spot, :].astype(jnp.float32)
+                    second = second_ref[row, spot, :].astype(jnp.float32)
+                    cells = jnp.where(swapped == (side == 0), first, second)
                 mask = fields[2 * rows + row : 2 * rows + row + 1, :]
                 east = speed_east + fields[row : row + 1, :]
                 north = speed_north + fields[rows + row : rows + row + 1, :]
@@ -234,7 +250,7 @@
                 to_north = jnp.maximum(north, 0.0)
                 stay = (1.0 - jnp.abs(east)) - jnp.abs(north)
                 coefs.append((stay, to_east, to_east - east, to_north, to_north - north))
-                energy.append(source[row, spot, :].astype(jnp.float32) * mask)
+                energy.append(cells * mask)
                 masks.append(mask)
         count = 3 * rows
         for step in range(SUBSTEPS):
@@ -258,8 +274,8 @@
     lax.fori_loop(0, bins // tile, one_tile, 0)
 
 
-def propagate(edges, below, own, above, fown, fbeside, fother, east, north):
-    rows, bins, cols = below.shape
+def propagate(edges, first, own, second, fown, fbeside, fother, east, north):
+    rows, bins, cols = first.shape
     return pl.pallas_call(
         propagate_body,
         out_shape=jax.ShapeDtypeStruct((2 * rows, bins, cols), jnp.bfloat16),
@@ -270,7 +286,7 @@
         compiler_params=pltpu.CompilerParams(vmem_limit_bytes=8 << 20),
         cost_estimate=pl.CostEstimate(flops=40_000_000, bytes_accessed=1_600_000, transcendentals=0),
         name="propagate",
-    )(edges, below, own, above, fown, fbeside, fother, east, north)
+    )(edges, first, own, second, fown, fbeside, fother, east, north)
 
 
 def finish_body(comp_ref, fragment_ref, source_ref, kernel_ref, wet_ref, updated_ref, stokes_ref):
@@ -345,23 +361,27 @@
         "wide", split_axis=0, concat_axis=0, tiled=True, axis_index_groups=far,
     )
     total = strips * wides
-    upward = [(i, i + ROWS) for i in range(total - ROWS)]
-    downward = [(i + ROWS, i) for i in range(total - ROWS)]
     chain = ("strip", "wide")
+
+    def swaps(start):
+        pairs = [(g * ROWS + i, g * ROWS + ROWS + i) for g in range(start, total // ROWS - 1, 2) for i in range(ROWS)]
+        return pairs + [(b, a) for a, b in pairs]
+
     bins = own[:, :share]
-    below = lax.ppermute(bins, chain, upward)
-    above = lax.ppermute(bins, chain, downward)
+    first = lax.ppermute(bins, chain, swaps(0))
+    second = lax.ppermute(bins, chain, swaps(1))
     fown = interpolate((1,), table, *fetched)
     crossing = [
         (s * wides + wides - ROWS + i, (s + 1) * wides + i) for s in range(strips - 1) for i in range(ROWS)
     ]
     fother = lax.ppermute(fown, chain, crossing + [(b, a) for a, b in crossing])
     fbeside = interpolate((0, 2), table, *fetched)
-    edges = jnp.stack([group_index == 0, group_index == groups - 1]).astype(jnp.int32)
+    chain_index = lax.axis_index("strip") * groups + group_index
+    edges = jnp.stack([group_index == 0, group_index == groups - 1, chain_index % 2 == 1]).astype(jnp.int32)
 
     first_bin = comp_index * local_bins + member * share
     east, north = bin_speeds(first_bin, share)
-    spread = propagate(edges, below, own, above, fown, fbeside, fother, east, north)
+    spread = propagate(edges, first, own, second, fown, fbeside, fother, east, north)
 
     both = [
         [(ROWS * g + i) * comps + k for k in range(comps) for i in range(ROWS)] for g in range(groups)

time: 79.8 us -> 80 us (level)
  local copies, waits for them, and re-layouts: 1.92 us -> 0.19 us
  Pallas kernels: 10.7 us -> 11.8 us
  starting transfers between devices: 31.3 us -> 32.2 us
    unnamed x11 -> x8, local copies, waits for them, and re-layouts: 1.75 us -> 0.02 us
    pallas_call x1, Pallas kernels: 0.84 us -> 1.79 us  [pack(): pl.pallas_call(pack_body, out_shape=jax.ShapeDtypeStruct((members, bins +...]
where the time goes in v4:
time: 80 us; the launch traced here: 79.6 us
  waiting for transfers between devices  34.1 us (43%)
  starting transfers between devices  32.2 us (40%)
  Pallas kernels  11.8 us (15%)
  between operations  0.85 us (1%)
    ppermute x1, starting transfers between devices, step(): second = lax.ppermute(bins, chain, swaps(1))  12.7 us
    all_to_all x1, waiting for transfers between devices, step(): lax.all_to_all(spread, ('wide', 'comp'), split_axis=0, concat_axis=0, til...  10.6 us
    all_to_all x1, waiting for transfers between devices, step(): lax.all_to_all(unpack(own, groups), 'wide', split_axis=0, concat_axis=0,...  10 us
    all_to_all x1, waiting for transfers between devices, step(): lax.all_to_all(message, 'wide', split_axis=0, concat_axis=0, tiled=True,...  8.03 us
    ppermute x1, waiting for transfers between devices, step(): fother = lax.ppermute(fown, chain, crossing + [(b, a) for a, b in crossing])  5.51 us
    pallas_call x1, Pallas kernels, propagate(): pl.pallas_call(propagate_body, out_shape=jax.ShapeDtypeStruct((2 * rows,...  5.2 us
    all_to_all x1, starting transfers between devices, step(): lax.all_to_all(unpack(own, groups), 'wide', split_axis=0, concat_axis=0,...  4.99 us
    all_to_all x1, starting transfers between devices, step(): lax.all_to_all(message, 'wide', split_axis=0, concat_axis=0, tiled=True,...  4.3 us
  transfers between devices with their start and end apart: 6, of which 4 were waited for; matrix products, arithmetic and copies ran while one was open for 1% of the time, Pallas kernels for 3%

profile of v4, /device:TPU:32, one launch (start us, length us, event | category | flops | bytes accessed | tf_op | source)
XLA Modules:
  0.0 79.6 jit_solution(18023742055249320861)
XLA Ops:
  0.6 0.0 copy-start.3
  0.6 0.0 copy-start.2
  0.7 0.0 copy-start.1
  0.7 1.8 %pack.1 = bf16[4,160,256]{2,1,0:T(8,128)(2,1)} custom-call(s32[1]{0:T(128)} %bitcast.4.place_ref, bf16[4,144,256]{2,1,0:T(8,128)(2,1)} %bitcast.13, f32[2,4,8]{2,1,0:T(4,128)} %bitcast.14), custom_call_target="tpu_custom_call" | custom-call | flops 100000 | bytes 700000 | tf_op jit(solution)/shard_map/pack/pallas_call | solution.py:82
  2.5 4.3 %all-to-all-start = ((bf16[4,160,256]{2,1,0:T(8,128)(2,1)}), bf16[4,160,256]{2,1,0:T(8,128)(2,1)S(1)}, u32[]{:S(2)}, u32[]{:S(2)}) async-start(bf16[4,160,256]{2,1,0:T(8,128)(2,1)} %pack.1), calls=%async_computation | async-start | bytes 655360 | tf_op jit(solution)/shard_map/all_to_all | solution.py:352
  6.8 0.0 copy-done.3
  6.8 0.1 sine_multiply_fusion
  6.9 0.1 fusion.13
  7.0 8.0 %all-to-all-done.own_ref = bf16[4,160,256]{2,1,0:T(8,128)(2,1)S(1)} async-done(((bf16[4,160,256]{2,1,0:T(8,128)(2,1)}), bf16[4,160,256]{2,1,0:T(8,128)(2,1)S(1)}, u32[]{:S(2)}, u32[]{:S(2)}) %all-to-all-start) | async-done | bytes 327712 | tf_op jit(solution)/shard_map/all_to_all | solution.py:352
  15.0 4.3 %collective-permute-start = (bf16[4,144,256]{2,1,0:T(8,128)(2,1)S(1)}, bf16[4,144,256]{2,1,0:T(8,128)(2,1)S(1)}, u32[]{:S(2)}, u32[]{:S(2)}) collective-permute-start(bf16[4,144,256]{2,1,0:T(8,128)(2,1)S(1)} %slice.4), channel_id=1, source_target_pairs={{0,8},{2,10},{4,12},{6,14},{16,24},{18,26},{20,28},{22,30},{32,40}... | collective-permute-start | bytes 884744 | tf_op jit(solution)/shard_map/ppermute | solution.py:371
  19.3 12.7 %collective-permute-start.1 = (bf16[4,144,256]{2,1,0:T(8,128)(2,1)S(1)}, bf16[4,144,256]{2,1,0:T(8,128)(2,1)S(1)}, u32[]{:S(2)}, u32[]{:S(2)}) collective-permute-start(bf16[4,144,256]{2,1,0:T(8,128)(2,1)S(1)} %slice.4), channel_id=1, source_target_pairs={{8,16},{10,18},{12,20},{14,22},{24,32},{26,34},{28,36},{30,38},{40... | collective-permute-start | bytes 884744 | tf_op jit(solution)/shard_map/ppermute | solution.py:372
  32.0 0.6 unpack.1
  32.6 5.0 %all-to-all-start.1 = ((f32[12,8,128]{2,1,0:T(8,128)}), f32[12,8,128]{2,1,0:T(8,128)S(1)}, u32[]{:S(2)}, u32[]{:S(2)}) async-start(f32[12,8,128]{2,1,0:T(8,128)} %unpack.1), calls=%async_computation.1 | async-start | bytes 98304 | tf_op jit(solution)/shard_map/all_to_all | solution.py:359
  37.6 0.1 pad_add_fusion.place_ref
  37.7 0.0 copy-done.2
  37.7 0.0 copy-done.1
  37.7 0.7 fetch.1
  38.4 10.0 %all-to-all-done.1.gathered_ref = f32[12,8,128]{2,1,0:T(8,128)S(1)} async-done(((f32[12,8,128]{2,1,0:T(8,128)}), f32[12,8,128]{2,1,0:T(8,128)S(1)}, u32[]{:S(2)}, u32[]{:S(2)}) %all-to-all-start.1) | async-done | bytes 49184 | tf_op jit(solution)/shard_map/all_to_all | solution.py:359
  48.4 0.5 interpolate.2.fown_ref
  48.9 2.5 %collective-permute-start.2 = (f32[16,256]{1,0:T(8,128)S(1)}, f32[16,256]{1,0:T(8,128)S(1)}, u32[]{:S(2)}, u32[]{:S(2)}) collective-permute-start(f32[16,256]{1,0:T(8,128)S(1)} %interpolate.2.fown_ref), channel_id=1, source_target_pairs={{88,96},{90,98},{92,100},{94,102},{184,192},{186,194},{188,196},{1... | collective-permute-start | bytes 49160 | tf_op jit(solution)/shard_map/ppermute | solution.py:377
  51.4 0.1 add_convert_fusion.edge_ref
  51.5 0.9 %interpolate.3.fbeside_ref = f32[32,256]{1,0:T(8,128)S(1)} custom-call(f32[12,8,128]{2,1,0:T(8,128)S(1)} %all-to-all-done.1.gathered_ref, s32[3,4,1024]{2,1,0:T(4,128)S(1)} %get-tuple-element.7.code_ref, f32[3,4,1024]{2,1,0:T(4,128)S(1)} %get-tuple-element.8.share_ref, f32[3,4,256]{2,1,0:T(4,128)S(1)} %get-tuple-element.9.wet_ref), custom_call_target="tpu_custom_call" | custom-call | flops 4000000 | bytes 200000 | tf_op jit(solution)/shard_map/interpolate/pallas_call | solution.py:207
  52.4 5.5 %collective-permute-done.2.fother_ref = f32[16,256]{1,0:T(8,128)S(1)} collective-permute-done((f32[16,256]{1,0:T(8,128)S(1)}, f32[16,256]{1,0:T(8,128)S(1)}, u32[]{:S(2)}, u32[]{:S(2)}) %collective-permute-start.2) | collective-permute-done | bytes 16416 | tf_op jit(solution)/shard_map/ppermute | solution.py:377
  57.9 0.0 collective-permute-done.first_ref
  57.9 0.0 collective-permute-done.1.second_ref
  57.9 0.1 broadcast_in_dim.4.east_ref
  58.0 0.1 broadcast_in_dim.5.north_ref
  58.0 0.0 copy-start
  58.0 5.2 %propagate.1 = bf16[8,144,256]{2,1,0:T(8,128)(2,1)} custom-call(s32[3]{0:T(128)S(1)} %add_convert_fusion.edge_ref, bf16[4,144,256]{2,1,0:T(8,128)(2,1)S(1)} %collective-permute-done.first_ref, bf16[4,160,256]{2,1,0:T(8,128)(2,1)S(1)} %all-to-all-done.own_ref, bf16[4,144,256]{2,1,0:T(8,128)(2,1)S(1)} %collective-permute-done.1.second_ref, ...), custom_call_target="tpu_custom_call" | custom-call | flops 40000000 | bytes 1600000 | tf_op jit(solution)/shard_map/propagate/pallas_call | solution.py:279
  63.2 3.5 %all-to-all-start.2 = ((bf16[8,144,256]{2,1,0:T(8,128)(2,1)}), bf16[8,144,256]{2,1,0:T(8,128)(2,1)S(1)}, u32[]{:S(2)}, u32[]{:S(2)}) async-start(bf16[8,144,256]{2,1,0:T(8,128)(2,1)} %propagate.1), calls=%async_computation.2 | async-start | bytes 1179648 | tf_op jit(solution)/shard_map/all_to_all | solution.py:389
  66.8 0.1 multiply_convert_fusion.1
  66.9 10.6 %all-to-all-done.2 = bf16[8,144,256]{2,1,0:T(8,128)(2,1)S(1)} async-done(((bf16[8,144,256]{2,1,0:T(8,128)(2,1)}), bf16[8,144,256]{2,1,0:T(8,128)(2,1)S(1)}, u32[]{:S(2)}, u32[]{:S(2)}) %all-to-all-start.2) | async-done | bytes 589856 | tf_op jit(solution)/shard_map/all_to_all | solution.py:389
  77.5 0.0 copy-done
  77.5 2.1 %finish.1 = (bf16[576,256]{1,0:T(8,128)(2,1)}, f32[32,256]{1,0:T(8,128)}) custom-call(s32[1]{0:T(128)} %bitcast.comp_ref, bf16[1152,256]{1,0:T(8,128)(2,1)S(1)} %bitcast.12, bf16[576,1152]{1,0:T(8,128)(2,1)S(1)} %copy-done, bf16[32,1152]{1,0:T(8,128)(2,1)S(1)} %pad_maximum_fusion.kernel_ref, f32[1,256]{1,0:T(1,128)S(1)} %dynamic-slice_convert_fusion.wet_ref), custom_call_target="tpu_custom_call" | custom-call | flops 358612992 | bytes 2500000 | tf_op jit(solution)/shard_map/finish/pallas_call | solution.py:312
  (5 shorter events, 0.1 us)
Async XLA Ops:
  0.6 6.2 %copy-start.3 = (s32[48,256]{1,0:T(8,128)S(1)}, s32[48,256]{1,0:T(8,128)}, u32[]{:S(2)}) copy-start(s32[48,256]{1,0:T(8,128)} %mask_ref.1) | copy-start | bytes 147460
  0.6 37.0 %copy-start.2 = (f32[4,12288]{1,0:T(4,128)S(1)}, f32[4,12288]{1,0:T(4,128)}, u32[]{:S(2)}) copy-start(f32[4,12288]{1,0:T(4,128)} %weight_ref.1) | copy-start | bytes 589828
  0.7 37.0 %copy-start.1 = (s32[4,12288]{1,0:T(4,128)S(1)}, s32[4,12288]{1,0:T(4,128)}, u32[]{:S(2)}) copy-start(s32[4,12288]{1,0:T(4,128)} %index_ref.1) | copy-start | bytes 589828
  2.5 12.5 %all-to-all-start = ((bf16[4,160,256]{2,1,0:T(8,128)(2,1)}), bf16[4,160,256]{2,1,0:T(8,128)(2,1)S(1)}, u32[]{:S(2)}, u32[]{:S(2)}) async-start(bf16[4,160,256]{2,1,0:T(8,128)(2,1)} %pack.1), calls=%async_computation | async-start | bytes 655360 | tf_op jit(solution)/shard_map/all_to_all | solution.py:352
  15.0 42.9 %collective-permute-start = (bf16[4,144,256]{2,1,0:T(8,128)(2,1)S(1)}, bf16[4,144,256]{2,1,0:T(8,128)(2,1)S(1)}, u32[]{:S(2)}, u32[]{:S(2)}) collective-permute-start(bf16[4,144,256]{2,1,0:T(8,128)(2,1)S(1)} %slice.4), channel_id=1, source_target_pairs={{0,8},{2,10},{4,12},{6,14},{16,24},{18,26},{20,28},{22,30},{32,40}... | collective-permute-start | bytes 884744 | tf_op jit(solution)/shard_map/ppermute | solution.py:371
  19.3 38.6 %collective-permute-start.1 = (bf16[4,144,256]{2,1,0:T(8,128)(2,1)S(1)}, bf16[4,144,256]{2,1,0:T(8,128)(2,1)S(1)}, u32[]{:S(2)}, u32[]{:S(2)}) collective-permute-start(bf16[4,144,256]{2,1,0:T(8,128)(2,1)S(1)} %slice.4), channel_id=1, source_target_pairs={{8,16},{10,18},{12,20},{14,22},{24,32},{26,34},{28,36},{30,38},{40... | collective-permute-start | bytes 884744 | tf_op jit(solution)/shard_map/ppermute | solution.py:372
  32.6 15.8 %all-to-all-start.1 = ((f32[12,8,128]{2,1,0:T(8,128)}), f32[12,8,128]{2,1,0:T(8,128)S(1)}, u32[]{:S(2)}, u32[]{:S(2)}) async-start(f32[12,8,128]{2,1,0:T(8,128)} %unpack.1), calls=%async_computation.1 | async-start | bytes 98304 | tf_op jit(solution)/shard_map/all_to_all | solution.py:359
  48.9 9.0 %collective-permute-start.2 = (f32[16,256]{1,0:T(8,128)S(1)}, f32[16,256]{1,0:T(8,128)S(1)}, u32[]{:S(2)}, u32[]{:S(2)}) collective-permute-start(f32[16,256]{1,0:T(8,128)S(1)} %interpolate.2.fown_ref), channel_id=1, source_target_pairs={{88,96},{90,98},{92,100},{94,102},{184,192},{186,194},{188,196},{1... | collective-permute-start | bytes 49160 | tf_op jit(solution)/shard_map/ppermute | solution.py:377
  58.0 19.4 %copy-start = (bf16[576,1152]{1,0:T(8,128)(2,1)S(1)}, bf16[576,1152]{1,0:T(8,128)(2,1)}, u32[]{:S(2)}) copy-start(bf16[576,1152]{1,0:T(8,128)(2,1)} %source_ref.1) | copy-start | bytes 3981316
  63.2 14.2 %all-to-all-start.2 = ((bf16[8,144,256]{2,1,0:T(8,128)(2,1)}), bf16[8,144,256]{2,1,0:T(8,128)(2,1)S(1)}, u32[]{:S(2)}, u32[]{:S(2)}) async-start(bf16[8,144,256]{2,1,0:T(8,128)(2,1)} %propagate.1), calls=%async_computation.2 | async-start | bytes 1179648 | tf_op jit(solution)/shard_map/all_to_all | solution.py:389

commit v5 on v4

--- a/solution.py
+++ b/solution.py
@@ -218,16 +218,28 @@
 
 
 def propagate_body(
-    edge_ref, first_ref, own_ref, second_ref, fown_ref, fbeside_ref, fother_ref, east_ref, north_ref,
+    edge_ref, first_ref, own_ref, second_ref, fields_ref, fother_ref, east_ref, north_ref,
     out_ref, fbelow_ref, fabove_ref,
 ):
-    rows, bins, cols = first_ref.shape
-    swapped = edge_ref[2] == 1
-    tile = 16
+    rows, bins, _ = first_ref.shape
     deep = 4 * rows
     fother = fother_ref[...]
-    fbelow_ref[...] = jnp.where(edge_ref[0] == 1, fother, fbeside_ref[0:deep, :])
-    fabove_ref[...] = jnp.where(edge_ref[1] == 1, fother, fbeside_ref[deep:, :])
+    fbelow_ref[...] = jnp.where(edge_ref[0] == 1, fother, fields_ref[0:deep, :])
+    fabove_ref[...] = jnp.where(edge_ref[1] == 1, fother, fields_ref[2 * deep :, :])
+    fields = (fbelow_ref, fields_ref.at[deep : 2 * deep, :], fabove_ref)
+
+    @pl.when(edge_ref[2] == 1)
+    def _():
+        substeps((first_ref, own_ref, second_ref), fields, east_ref, north_ref, out_ref, bins)
+
+    @pl.when(edge_ref[2] != 1)
+    def _():
+        substeps((second_ref, own_ref, first_ref), fields, east_ref, north_ref, out_ref, bins)
+
+
+def substeps(sources, all_fields, east_ref, north_ref, out_ref, bins):
+    rows, _, cols = sources[1].shape
+    tile = 16
 
     def one_tile(t, carry):
         spot = pl.ds(pl.multiple_of(t * tile, tile), tile)
@@ -235,14 +247,8 @@
         speed_north = jnp.concatenate([north_ref[spot, :]] * (cols // 128), 1)
         energy, masks = [], []
         coefs = []
-        for side, fields in enumerate((fbelow_ref, fown_ref, fabove_ref)):
+        for source, fields in zip(sources, all_fields):
             for row in range(rows):
-                if side == 1:
-                    cells = own_ref[row, spot, :].astype(jnp.float32)
-                else:
-                    first = first_ref[row, spot, :].astype(jnp.float32)
-                    second = second_ref[row, spot, :].astype(jnp.float32)
-                    cells = jnp.where(swapped == (side == 0), first, second)
                 mask = fields[2 * rows + row : 2 * rows + row + 1, :]
                 east = speed_east + fields[row : row + 1, :]
                 north = speed_north + fields[rows + row : rows + row + 1, :]
@@ -250,7 +256,7 @@
                 to_north = jnp.maximum(north, 0.0)
                 stay = (1.0 - jnp.abs(east)) - jnp.abs(north)
                 coefs.append((stay, to_east, to_east - east, to_north, to_north - north))
-                energy.append(cells * mask)
+                energy.append(source[row, spot, :].astype(jnp.float32) * mask)
                 masks.append(mask)
         count = 3 * rows
         for step in range(SUBSTEPS):
@@ -274,19 +280,19 @@
     lax.fori_loop(0, bins // tile, one_tile, 0)
 
 
-def propagate(edges, first, own, second, fown, fbeside, fother, east, north):
+def propagate(edges, first, own, second, fields, fother, east, north):
     rows, bins, cols = first.shape
     return pl.pallas_call(
         propagate_body,
         out_shape=jax.ShapeDtypeStruct((2 * rows, bins, cols), jnp.bfloat16),
         in_specs=[pl.BlockSpec(memory_space=pltpu.SMEM)]
-        + [pl.BlockSpec(memory_space=pltpu.VMEM)] * 8,
+        + [pl.BlockSpec(memory_space=pltpu.VMEM)] * 7,
         out_specs=pl.BlockSpec(memory_space=pltpu.VMEM),
         scratch_shapes=[pltpu.VMEM((4 * rows, cols), jnp.float32)] * 2,
         compiler_params=pltpu.CompilerParams(vmem_limit_bytes=8 << 20),
         cost_estimate=pl.CostEstimate(flops=40_000_000, bytes_accessed=1_600_000, transcendentals=0),
         name="propagate",
-    )(edges, first, own, second, fown, fbeside, fother, east, north)
+    )(edges, first, own, second, fields, fother, east, north)
 
 
 def finish_body(comp_ref, fragment_ref, source_ref, kernel_ref, wet_ref, updated_ref, stokes_ref):
@@ -307,7 +313,7 @@
     bins, points = fragment.shape
     local_bins = source_matrix.shape[0]
     levels = kernel.shape[0]
-    steps = 3
+    steps = 1
     tile = local_bins // steps
     return pl.pallas_call(
         finish_body,
@@ -352,8 +358,14 @@
     own = lax.all_to_all(
         message, "wide", split_axis=0, concat_axis=0, tiled=True, axis_index_groups=near
     )
+    lowest, highest = group_index == 0, group_index == groups - 1
     places = jnp.stack(
-        [jnp.maximum(group_index - 1, 0), group_index, jnp.minimum(group_index + 1, groups - 1)]
+        [
+            jnp.maximum(group_index - 1, 0),
+            group_index,
+            jnp.minimum(group_index + 1, groups - 1),
+            jnp.where(lowest, groups - 1, 0),
+        ]
     )
     fetched = fetch(places, remap_index, remap_weights, wet_mask)
     table = lax.all_to_all(
@@ -370,18 +382,20 @@
     bins = own[:, :share]
     first = lax.ppermute(bins, chain, swaps(0))
     second = lax.ppermute(bins, chain, swaps(1))
-    fown = interpolate((1,), table, *fetched)
-    crossing = [
-        (s * wides + wides - ROWS + i, (s + 1) * wides + i) for s in range(strips - 1) for i in range(ROWS)
-    ]
-    fother = lax.ppermute(fown, chain, crossing + [(b, a) for a, b in crossing])
-    fbeside = interpolate((0, 2), table, *fetched)
+    fedge = interpolate((3,), table, *fetched)
+    edge_moves = []
+    for s in range(strips - 1):
+        for i in range(ROWS):
+            last = wides - ROWS + i
+            edge_moves += [(s * wides + i, (s + 1) * wides + i), ((s + 1) * wides + last, s * wides + last)]
+    fother = lax.ppermute(fedge, chain, edge_moves)
+    fields = interpolate((0, 1, 2), table, *fetched)
     chain_index = lax.axis_index("strip") * groups + group_index
-    edges = jnp.stack([group_index == 0, group_index == groups - 1, chain_index % 2 == 1]).astype(jnp.int32)
+    edges = jnp.stack([lowest, highest, chain_index % 2 == 1]).astype(jnp.int32)
 
     first_bin = comp_index * local_bins + member * share
     east, north = bin_speeds(first_bin, share)
-    spread = propagate(edges, first, own, second, fown, fbeside, fother, east, north)
+    spread = propagate(edges, first, own, second, fields, fother, east, north)
 
     both = [
         [(ROWS * g + i) * comps + k for k in range(comps) for i in range(ROWS)] for g in range(groups)

time: 80 us -> 77 us (0.963)
  waiting for transfers between devices: 34.1 us -> 31.5 us
    ppermute x1, waiting for transfers between devices: 5.51 us -> 2.87 us  [step(): fother = lax.ppermute(fedge, chain, edge_moves)]
  transfers between devices with their start and end apart: 6 -> 6, of which waited for: 4 -> 4; matrix products, arithmetic and copies ran while one was open for 1% -> 1% of each run, Pallas kernels for 3% -> 4%
where the time goes in v5:
time: 77 us; the launch traced here: 76.6 us
  starting transfers between devices  32.3 us (42%)
  waiting for transfers between devices  31.5 us (41%)
  Pallas kernels  11.4 us (15%)
  between operations  0.85 us (1%)
    ppermute x1, starting transfers between devices, step(): second = lax.ppermute(bins, chain, swaps(1))  12.7 us
    all_to_all x1, waiting for transfers between devices, step(): lax.all_to_all(spread, ('wide', 'comp'), split_axis=0, concat_axis=0, til...  10.6 us
    all_to_all x1, waiting for transfers between devices, step(): lax.all_to_all(unpack(own, groups), 'wide', split_axis=0, concat_axis=0,...  10 us
    all_to_all x1, waiting for transfers between devices, step(): lax.all_to_all(message, 'wide', split_axis=0, concat_axis=0, tiled=True,...  8.02 us
    pallas_call x1, Pallas kernels, propagate(): pl.pallas_call(propagate_body, out_shape=jax.ShapeDtypeStruct((2 * rows,...  5.12 us
    all_to_all x1, starting transfers between devices, step(): lax.all_to_all(unpack(own, groups), 'wide', split_axis=0, concat_axis=0,...  4.99 us
    all_to_all x1, starting transfers between devices, step(): lax.all_to_all(message, 'wide', split_axis=0, concat_axis=0, tiled=True,...  4.3 us
    ppermute x1, starting transfers between devices, step(): first = lax.ppermute(bins, chain, swaps(0))  4.28 us
  transfers between devices with their start and end apart: 6, of which 4 were waited for; matrix products, arithmetic and copies ran while one was open for 1% of the time, Pallas kernels for 4%

profile of v5, /device:TPU:32, one launch (start us, length us, event | category | flops | bytes accessed | tf_op | source)
XLA Modules:
  0.0 76.6 jit_solution(2498876157032522287)
XLA Ops:
  0.6 0.0 copy-start.3
  0.6 0.0 copy-start.2
  0.7 0.0 copy-start.1
  0.7 1.8 %pack.1 = bf16[4,160,256]{2,1,0:T(8,128)(2,1)} custom-call(s32[1]{0:T(128)} %bitcast.4.place_ref, bf16[4,144,256]{2,1,0:T(8,128)(2,1)} %bitcast.14, f32[2,4,8]{2,1,0:T(4,128)} %bitcast.15), custom_call_target="tpu_custom_call" | custom-call | flops 100000 | bytes 700000 | tf_op jit(solution)/shard_map/pack/pallas_call | solution.py:82
  2.5 4.3 %all-to-all-start = ((bf16[4,160,256]{2,1,0:T(8,128)(2,1)}), bf16[4,160,256]{2,1,0:T(8,128)(2,1)S(1)}, u32[]{:S(2)}, u32[]{:S(2)}) async-start(bf16[4,160,256]{2,1,0:T(8,128)(2,1)} %pack.1), calls=%async_computation | async-start | bytes 655360 | tf_op jit(solution)/shard_map/all_to_all | solution.py:358
  6.8 0.0 copy-done.3
  6.8 0.1 sine_multiply_fusion
  6.9 0.1 fusion.13
  7.0 8.0 %all-to-all-done.own_ref = bf16[4,160,256]{2,1,0:T(8,128)(2,1)S(1)} async-done(((bf16[4,160,256]{2,1,0:T(8,128)(2,1)}), bf16[4,160,256]{2,1,0:T(8,128)(2,1)S(1)}, u32[]{:S(2)}, u32[]{:S(2)}) %all-to-all-start) | async-done | bytes 327712 | tf_op jit(solution)/shard_map/all_to_all | solution.py:358
  15.0 4.3 %collective-permute-start = (bf16[4,144,256]{2,1,0:T(8,128)(2,1)S(1)}, bf16[4,144,256]{2,1,0:T(8,128)(2,1)S(1)}, u32[]{:S(2)}, u32[]{:S(2)}) collective-permute-start(bf16[4,144,256]{2,1,0:T(8,128)(2,1)S(1)} %slice.4), channel_id=1, source_target_pairs={{0,8},{2,10},{4,12},{6,14},{16,24},{18,26},{20,28},{22,30},{32,40}... | collective-permute-start | bytes 884744 | tf_op jit(solution)/shard_map/ppermute | solution.py:383
  19.3 12.7 %collective-permute-start.1 = (bf16[4,144,256]{2,1,0:T(8,128)(2,1)S(1)}, bf16[4,144,256]{2,1,0:T(8,128)(2,1)S(1)}, u32[]{:S(2)}, u32[]{:S(2)}) collective-permute-start(bf16[4,144,256]{2,1,0:T(8,128)(2,1)S(1)} %slice.4), channel_id=1, source_target_pairs={{8,16},{10,18},{12,20},{14,22},{24,32},{26,34},{28,36},{30,38},{40... | collective-permute-start | bytes 884744 | tf_op jit(solution)/shard_map/ppermute | solution.py:384
  32.0 0.6 unpack.1
  32.6 5.0 %all-to-all-start.1 = ((f32[12,8,128]{2,1,0:T(8,128)}), f32[12,8,128]{2,1,0:T(8,128)S(1)}, u32[]{:S(2)}, u32[]{:S(2)}) async-start(f32[12,8,128]{2,1,0:T(8,128)} %unpack.1), calls=%async_computation.1 | async-start | bytes 98304 | tf_op jit(solution)/shard_map/all_to_all | solution.py:371
  37.6 0.1 pad_add_fusion.place_ref
  37.7 0.0 copy-done.2
  37.7 0.0 copy-done.1
  37.7 0.7 fetch.1
  38.4 10.0 %all-to-all-done.1.gathered_ref = f32[12,8,128]{2,1,0:T(8,128)S(1)} async-done(((f32[12,8,128]{2,1,0:T(8,128)}), f32[12,8,128]{2,1,0:T(8,128)S(1)}, u32[]{:S(2)}, u32[]{:S(2)}) %all-to-all-start.1) | async-done | bytes 49184 | tf_op jit(solution)/shard_map/all_to_all | solution.py:371
  48.4 0.5 interpolate.3
  48.9 2.6 %collective-permute-start.2 = (f32[16,256]{1,0:T(8,128)S(1)}, f32[16,256]{1,0:T(8,128)S(1)}, u32[]{:S(2)}, u32[]{:S(2)}) collective-permute-start(f32[16,256]{1,0:T(8,128)S(1)} %interpolate.3), channel_id=1, source_target_pairs={{0,96},{184,88},{2,98},{186,90},{4,100},{188,92},{6,102},{190,94},... | collective-permute-start | bytes 49160 | tf_op jit(solution)/shard_map/ppermute | solution.py:391
  51.5 0.1 add_convert_fusion.edge_ref
  51.6 1.3 %interpolate.2.fields_ref = f32[48,256]{1,0:T(8,128)S(1)} custom-call(f32[12,8,128]{2,1,0:T(8,128)S(1)} %all-to-all-done.1.gathered_ref, s32[4,4,1024]{2,1,0:T(4,128)S(1)} %get-tuple-element.7.code_ref, f32[4,4,1024]{2,1,0:T(4,128)S(1)} %get-tuple-element.8.share_ref, f32[4,4,256]{2,1,0:T(4,128)S(1)} %get-tuple-element.9.wet_ref), custom_call_target="tpu_custom_call" | custom-call | flops 6000000 | bytes 300000 | tf_op jit(solution)/shard_map/interpolate/pallas_call | solution.py:207
  52.9 2.9 %collective-permute-done.2.fother_ref = f32[16,256]{1,0:T(8,128)S(1)} collective-permute-done((f32[16,256]{1,0:T(8,128)S(1)}, f32[16,256]{1,0:T(8,128)S(1)}, u32[]{:S(2)}, u32[]{:S(2)}) %collective-permute-start.2) | collective-permute-done | bytes 16416 | tf_op jit(solution)/shard_map/ppermute | solution.py:391
  55.8 0.0 collective-permute-done.first_ref
  55.8 0.0 collective-permute-done.1.second_ref
  55.8 0.1 broadcast_in_dim.4.east_ref
  55.8 0.1 broadcast_in_dim.5.north_ref
  55.9 0.0 copy-start
  55.9 5.1 %propagate.1 = bf16[8,144,256]{2,1,0:T(8,128)(2,1)} custom-call(s32[3]{0:T(128)S(1)} %add_convert_fusion.edge_ref, bf16[4,144,256]{2,1,0:T(8,128)(2,1)S(1)} %collective-permute-done.first_ref, bf16[4,160,256]{2,1,0:T(8,128)(2,1)S(1)} %all-to-all-done.own_ref, bf16[4,144,256]{2,1,0:T(8,128)(2,1)S(1)} %collective-permute-done.1.second_ref, ...), custom_call_target="tpu_custom_call" | custom-call | flops 40000000 | bytes 1600000 | tf_op jit(solution)/shard_map/propagate/pallas_call | solution.py:285
  61.1 3.5 %all-to-all-start.2 = ((bf16[8,144,256]{2,1,0:T(8,128)(2,1)}), bf16[8,144,256]{2,1,0:T(8,128)(2,1)S(1)}, u32[]{:S(2)}, u32[]{:S(2)}) async-start(bf16[8,144,256]{2,1,0:T(8,128)(2,1)} %propagate.1), calls=%async_computation.2 | async-start | bytes 1179648 | tf_op jit(solution)/shard_map/all_to_all | solution.py:403
  64.6 0.1 multiply_convert_fusion.1
  64.7 10.6 %all-to-all-done.2 = bf16[8,144,256]{2,1,0:T(8,128)(2,1)S(1)} async-done(((bf16[8,144,256]{2,1,0:T(8,128)(2,1)}), bf16[8,144,256]{2,1,0:T(8,128)(2,1)S(1)}, u32[]{:S(2)}, u32[]{:S(2)}) %all-to-all-start.2) | async-done | bytes 589856 | tf_op jit(solution)/shard_map/all_to_all | solution.py:403
  75.3 0.0 copy-done
  75.3 1.3 %finish.1 = (bf16[576,256]{1,0:T(8,128)(2,1)}, f32[32,256]{1,0:T(8,128)}) custom-call(s32[1]{0:T(128)} %bitcast.comp_ref, bf16[1152,256]{1,0:T(8,128)(2,1)S(1)} %bitcast.13, bf16[576,1152]{1,0:T(8,128)(2,1)S(1)} %copy-done, bf16[32,1152]{1,0:T(8,128)(2,1)S(1)} %pad_maximum_fusion.kernel_ref, f32[1,256]{1,0:T(1,128)S(1)} %dynamic-slice_convert_fusion.wet_ref), custom_call_target="tpu_custom_call" | custom-call | flops 358612992 | bytes 2500000 | tf_op jit(solution)/shard_map/finish/pallas_call | solution.py:318
  (5 shorter events, 0.1 us)
Async XLA Ops:
  0.6 6.2 %copy-start.3 = (s32[48,256]{1,0:T(8,128)S(1)}, s32[48,256]{1,0:T(8,128)}, u32[]{:S(2)}) copy-start(s32[48,256]{1,0:T(8,128)} %mask_ref.1) | copy-start | bytes 147460
  0.6 37.0 %copy-start.2 = (f32[4,12288]{1,0:T(4,128)S(1)}, f32[4,12288]{1,0:T(4,128)}, u32[]{:S(2)}) copy-start(f32[4,12288]{1,0:T(4,128)} %weight_ref.1) | copy-start | bytes 589828
  0.7 37.0 %copy-start.1 = (s32[4,12288]{1,0:T(4,128)S(1)}, s32[4,12288]{1,0:T(4,128)}, u32[]{:S(2)}) copy-start(s32[4,12288]{1,0:T(4,128)} %index_ref.1) | copy-start | bytes 589828
  2.5 12.5 %all-to-all-start = ((bf16[4,160,256]{2,1,0:T(8,128)(2,1)}), bf16[4,160,256]{2,1,0:T(8,128)(2,1)S(1)}, u32[]{:S(2)}, u32[]{:S(2)}) async-start(bf16[4,160,256]{2,1,0:T(8,128)(2,1)} %pack.1), calls=%async_computation | async-start | bytes 655360 | tf_op jit(solution)/shard_map/all_to_all | solution.py:358
  15.0 40.7 %collective-permute-start = (bf16[4,144,256]{2,1,0:T(8,128)(2,1)S(1)}, bf16[4,144,256]{2,1,0:T(8,128)(2,1)S(1)}, u32[]{:S(2)}, u32[]{:S(2)}) collective-permute-start(bf16[4,144,256]{2,1,0:T(8,128)(2,1)S(1)} %slice.4), channel_id=1, source_target_pairs={{0,8},{2,10},{4,12},{6,14},{16,24},{18,26},{20,28},{22,30},{32,40}... | collective-permute-start | bytes 884744 | tf_op jit(solution)/shard_map/ppermute | solution.py:383
  19.3 36.5 %collective-permute-start.1 = (bf16[4,144,256]{2,1,0:T(8,128)(2,1)S(1)}, bf16[4,144,256]{2,1,0:T(8,128)(2,1)S(1)}, u32[]{:S(2)}, u32[]{:S(2)}) collective-permute-start(bf16[4,144,256]{2,1,0:T(8,128)(2,1)S(1)} %slice.4), channel_id=1, source_target_pairs={{8,16},{10,18},{12,20},{14,22},{24,32},{26,34},{28,36},{30,38},{40... | collective-permute-start | bytes 884744 | tf_op jit(solution)/shard_map/ppermute | solution.py:384
  32.6 15.8 %all-to-all-start.1 = ((f32[12,8,128]{2,1,0:T(8,128)}), f32[12,8,128]{2,1,0:T(8,128)S(1)}, u32[]{:S(2)}, u32[]{:S(2)}) async-start(f32[12,8,128]{2,1,0:T(8,128)} %unpack.1), calls=%async_computation.1 | async-start | bytes 98304 | tf_op jit(solution)/shard_map/all_to_all | solution.py:371
  48.9 6.8 %collective-permute-start.2 = (f32[16,256]{1,0:T(8,128)S(1)}, f32[16,256]{1,0:T(8,128)S(1)}, u32[]{:S(2)}, u32[]{:S(2)}) collective-permute-start(f32[16,256]{1,0:T(8,128)S(1)} %interpolate.3), channel_id=1, source_target_pairs={{0,96},{184,88},{2,98},{186,90},{4,100},{188,92},{6,102},{190,94},... | collective-permute-start | bytes 49160 | tf_op jit(solution)/shard_map/ppermute | solution.py:391
  55.9 19.3 %copy-start = (bf16[576,1152]{1,0:T(8,128)(2,1)S(1)}, bf16[576,1152]{1,0:T(8,128)(2,1)}, u32[]{:S(2)}) copy-start(bf16[576,1152]{1,0:T(8,128)(2,1)} %source_ref.1) | copy-start | bytes 3981316
  61.1 14.2 %all-to-all-start.2 = ((bf16[8,144,256]{2,1,0:T(8,128)(2,1)}), bf16[8,144,256]{2,1,0:T(8,128)(2,1)S(1)}, u32[]{:S(2)}, u32[]{:S(2)}) async-start(bf16[8,144,256]{2,1,0:T(8,128)(2,1)} %propagate.1), calls=%async_computation.2 | async-start | bytes 1179648 | tf_op jit(solution)/shard_map/all_to_all | solution.py:403

commit v6 on v5

--- a/solution.py
+++ b/solution.py
@@ -165,13 +165,19 @@
     )(places, remap_index, remap_weights, wet_mask)
 
 
+def visit_order(groups):
+    half = groups // 2
+    return [g // 2 + (g % 2) * half for g in range(groups)] if groups % 2 == 0 else list(range(groups))
+
+
 def interpolate_body(blocks, gathered_ref, code_ref, share_ref, wet_ref, out_ref):
     groups = gathered_ref.shape[0]
     rows, cols = wet_ref.shape[1:]
     row_ids = lax.broadcasted_iota(jnp.int32, (OCEAN_ROWS, 128), 0)
+    order = visit_order(groups)
     tables = []
     for part in range(groups // 4):
-        pieces = [gathered_ref[4 * part + i] for i in range(4)]
+        pieces = [gathered_ref[order.index(4 * part + i)] for i in range(4)]
         tables.append((pieces[0] + pieces[1]) + (pieces[2] + pieces[3]))
     for place, block in enumerate(blocks):
         base = place * 4 * rows
@@ -219,9 +225,9 @@
 
 def propagate_body(
     edge_ref, first_ref, own_ref, second_ref, fields_ref, fother_ref, east_ref, north_ref,
-    out_ref, fbelow_ref, fabove_ref,
+    out_ref, fbelow_ref, fabove_ref, ready_ref, done,
 ):
-    rows, bins, _ = first_ref.shape
+    rows, _, _ = first_ref.shape
     deep = 4 * rows
     fother = fother_ref[...]
     fbelow_ref[...] = jnp.where(edge_ref[0] == 1, fother, fields_ref[0:deep, :])
@@ -230,16 +236,21 @@
 
     @pl.when(edge_ref[2] == 1)
     def _():
-        substeps((first_ref, own_ref, second_ref), fields, east_ref, north_ref, out_ref, bins)
+        substeps((first_ref, own_ref, second_ref), fields, east_ref, north_ref, out_ref, ready_ref, done)
 
     @pl.when(edge_ref[2] != 1)
     def _():
-        substeps((second_ref, own_ref, first_ref), fields, east_ref, north_ref, out_ref, bins)
-
-
-def substeps(sources, all_fields, east_ref, north_ref, out_ref, bins):
+        substeps((second_ref, own_ref, first_ref), fields, east_ref, north_ref, out_ref, ready_ref, done)
+
+
+def substeps(sources, all_fields, east_ref, north_ref, out_ref, ready_ref, done):
     rows, _, cols = sources[1].shape
+    bins = out_ref.shape[1]
     tile = 16
+
+    def copy_out(t):
+        spot = pl.ds(pl.multiple_of(t * tile, tile), tile)
+        return pltpu.make_async_copy(ready_ref.at[:, spot, :], out_ref.at[:, spot, :], done.at[t])
 
     def one_tile(t, carry):
         spot = pl.ds(pl.multiple_of(t * tile, tile), tile)
@@ -273,11 +284,14 @@
             energy = fresh
         for row in range(rows):
             result = energy[rows + row].astype(jnp.bfloat16)
-            out_ref[row, spot, :] = result
-            out_ref[rows + row, spot, :] = result
+            ready_ref[row, spot, :] = result
+            ready_ref[rows + row, spot, :] = result
+        copy_out(t).start()
         return carry
 
     lax.fori_loop(0, bins // tile, one_tile, 0)
+    for t in range(bins // tile):
+        copy_out(t).wait()
 
 
 def propagate(edges, first, own, second, fields, fother, east, north):
@@ -287,51 +301,63 @@
         out_shape=jax.ShapeDtypeStruct((2 * rows, bins, cols), jnp.bfloat16),
         in_specs=[pl.BlockSpec(memory_space=pltpu.SMEM)]
         + [pl.BlockSpec(memory_space=pltpu.VMEM)] * 7,
-        out_specs=pl.BlockSpec(memory_space=pltpu.VMEM),
-        scratch_shapes=[pltpu.VMEM((4 * rows, cols), jnp.float32)] * 2,
+        out_specs=pl.BlockSpec(memory_space=pltpu.HBM),
+        scratch_shapes=[pltpu.VMEM((4 * rows, cols), jnp.float32)] * 2
+        + [
+            pltpu.VMEM((2 * rows, bins, cols), jnp.bfloat16),
+            pltpu.SemaphoreType.DMA((bins // 16,)),
+        ],
         compiler_params=pltpu.CompilerParams(vmem_limit_bytes=8 << 20),
         cost_estimate=pl.CostEstimate(flops=40_000_000, bytes_accessed=1_600_000, transcendentals=0),
         name="propagate",
     )(edges, first, own, second, fields, fother, east, north)
 
 
-def finish_body(comp_ref, fragment_ref, source_ref, kernel_ref, wet_ref, updated_ref, stokes_ref):
+def finish_body(
+    comp_ref, fragment_ref, source_ref, kernel_ref, wet_ref, updated_ref, stokes_ref, new_ref, drift_ref, done
+):
     rows = updated_ref.shape[0]
-    steps = pl.num_programs(0)
+    parts = 4
+    tile = rows // parts
     fragment = fragment_ref[...]
-    source = jnp.dot(source_ref[...], fragment, preferred_element_type=jnp.float32)
-    first = (comp_ref[0] * steps + pl.program_id(0)) * rows
-    returned = fragment_ref[pl.ds(pl.multiple_of(first, 16), rows), :].astype(jnp.float32)
-    updated_ref[...] = (wet_ref[...] * jnp.maximum(returned + source, 0.0)).astype(jnp.bfloat16)
-
-    @pl.when(pl.program_id(0) == 0)
-    def _():
-        stokes_ref[...] = jnp.dot(kernel_ref[...], fragment, preferred_element_type=jnp.float32)
+    copies = []
+    for part in range(parts):
+        spot = slice(part * tile, part * tile + tile)
+        source = jnp.dot(source_ref[spot, :], fragment, preferred_element_type=jnp.float32)
+        first = pl.multiple_of(comp_ref[0] * rows + part * tile, 16)
+        returned = fragment_ref[pl.ds(first, tile), :].astype(jnp.float32)
+        new_ref[spot, :] = (wet_ref[...] * jnp.maximum(returned + source, 0.0)).astype(jnp.bfloat16)
+        copies.append(
+            pltpu.make_async_copy(
+                new_ref.at[pl.ds(part * tile, tile), :], updated_ref.at[pl.ds(part * tile, tile), :], done.at[part]
+            )
+        )
+        copies[-1].start()
+        if part == parts - 2:
+            drift_ref[...] = jnp.dot(kernel_ref[...], fragment, preferred_element_type=jnp.float32)
+            copies.append(pltpu.make_async_copy(drift_ref, stokes_ref, done.at[parts]))
+            copies[-1].start()
+    for copy in copies:
+        copy.wait()
 
 
 def finish(comp_index, fragment, source_matrix, kernel, wet_points):
     bins, points = fragment.shape
     local_bins = source_matrix.shape[0]
     levels = kernel.shape[0]
-    steps = 1
-    tile = local_bins // steps
     return pl.pallas_call(
         finish_body,
-        grid=(steps,),
         out_shape=[
             jax.ShapeDtypeStruct((local_bins, points), jnp.bfloat16),
             jax.ShapeDtypeStruct((levels, points), jnp.float32),
         ],
-        in_specs=[
-            pl.BlockSpec(memory_space=pltpu.SMEM),
-            pl.BlockSpec((bins, points), lambda i: (0, 0)),
-            pl.BlockSpec((tile, bins), lambda i: (i, 0)),
-            pl.BlockSpec((levels, bins), lambda i: (0, 0)),
-            pl.BlockSpec((1, points), lambda i: (0, 0)),
-        ],
-        out_specs=[
-            pl.BlockSpec((tile, points), lambda i: (i, 0)),
-            pl.BlockSpec((levels, points), lambda i: (0, 0)),
+        in_specs=[pl.BlockSpec(memory_space=pltpu.SMEM)]
+        + [pl.BlockSpec(memory_space=pltpu.VMEM)] * 4,
+        out_specs=[pl.BlockSpec(memory_space=pltpu.HBM)] * 2,
+        scratch_shapes=[
+            pltpu.VMEM((local_bins, points), jnp.bfloat16),
+            pltpu.VMEM((levels, points), jnp.float32),
+            pltpu.SemaphoreType.DMA((5,)),
         ],
         compiler_params=pltpu.CompilerParams(vmem_limit_bytes=8 << 20),
         cost_estimate=pl.CostEstimate(
@@ -352,7 +378,7 @@
     member = wide_index % ROWS
     share = local_bins // ROWS
     near = [[ROWS * g + i for i in range(ROWS)] for g in range(groups)]
-    far = [[ROWS * g + i for g in range(groups)] for i in range(ROWS)]
+    far = [[ROWS * g + i for g in visit_order(groups)] for i in range(ROWS)]
 
     message = pack((wide_index % 16).reshape(1), spectrum.reshape(ROWS, share, points), currents)
     own = lax.all_to_all(

time: 77 us -> 76.5 us (level)
  no operation moved by 1% of the time
where the time goes in v6:
time: 76.5 us; the launch traced here: 76.1 us
  starting transfers between devices  32.4 us (42%)
  waiting for transfers between devices  31 us (41%)
  Pallas kernels  11.3 us (15%)
  between operations  0.86 us (1%)
    ppermute x1, starting transfers between devices, step(): second = lax.ppermute(bins, chain, swaps(1))  12.7 us
    all_to_all x1, waiting for transfers between devices, step(): lax.all_to_all(spread, ('wide', 'comp'), split_axis=0, concat_axis=0, til...  10.6 us
    all_to_all x1, waiting for transfers between devices, step(): lax.all_to_all(unpack(own, groups), 'wide', split_axis=0, concat_axis=0,...  9.54 us
    all_to_all x1, waiting for transfers between devices, step(): lax.all_to_all(message, 'wide', split_axis=0, concat_axis=0, tiled=True,...  8.02 us
    pallas_call x1, Pallas kernels, propagate(): pl.pallas_call(propagate_body, out_shape=jax.ShapeDtypeStruct((2 * rows,...  5.02 us
    all_to_all x1, starting transfers between devices, step(): lax.all_to_all(unpack(own, groups), 'wide', split_axis=0, concat_axis=0,...  4.99 us
    all_to_all x1, starting transfers between devices, step(): lax.all_to_all(message, 'wide', split_axis=0, concat_axis=0, tiled=True,...  4.3 us
    ppermute x1, starting transfers between devices, step(): first = lax.ppermute(bins, chain, swaps(0))  4.28 us
  transfers between devices with their start and end apart: 6, of which 4 were waited for; matrix products, arithmetic and copies ran while one was open for 1% of the time, Pallas kernels for 4%

profile of v6, /device:TPU:32, one launch (start us, length us, event | category | flops | bytes accessed | tf_op | source)
XLA Modules:
  0.0 76.1 jit_solution(6932032001960797202)
XLA Ops:
  0.6 0.0 copy-start.3
  0.6 0.0 copy-start.2
  0.7 0.0 copy-start.1
  0.7 1.8 %pack.1 = bf16[4,160,256]{2,1,0:T(8,128)(2,1)} custom-call(s32[1]{0:T(128)} %bitcast.4.place_ref, bf16[4,144,256]{2,1,0:T(8,128)(2,1)} %bitcast.14, f32[2,4,8]{2,1,0:T(4,128)} %bitcast.15), custom_call_target="tpu_custom_call" | custom-call | flops 100000 | bytes 700000 | tf_op jit(solution)/shard_map/pack/pallas_call | solution.py:82
  2.5 4.3 %all-to-all-start = ((bf16[4,160,256]{2,1,0:T(8,128)(2,1)}), bf16[4,160,256]{2,1,0:T(8,128)(2,1)S(1)}, u32[]{:S(2)}, u32[]{:S(2)}) async-start(bf16[4,160,256]{2,1,0:T(8,128)(2,1)} %pack.1), calls=%async_computation | async-start | bytes 655360 | tf_op jit(solution)/shard_map/all_to_all | solution.py:384
  6.8 0.0 copy-done.3
  6.8 0.1 sine_multiply_fusion
  6.9 0.1 fusion.13
  7.0 8.0 %all-to-all-done.own_ref = bf16[4,160,256]{2,1,0:T(8,128)(2,1)S(1)} async-done(((bf16[4,160,256]{2,1,0:T(8,128)(2,1)}), bf16[4,160,256]{2,1,0:T(8,128)(2,1)S(1)}, u32[]{:S(2)}, u32[]{:S(2)}) %all-to-all-start) | async-done | bytes 327712 | tf_op jit(solution)/shard_map/all_to_all | solution.py:384
  15.0 4.3 %collective-permute-start = (bf16[4,144,256]{2,1,0:T(8,128)(2,1)S(1)}, bf16[4,144,256]{2,1,0:T(8,128)(2,1)S(1)}, u32[]{:S(2)}, u32[]{:S(2)}) collective-permute-start(bf16[4,144,256]{2,1,0:T(8,128)(2,1)S(1)} %slice.4), channel_id=1, source_target_pairs={{0,8},{2,10},{4,12},{6,14},{16,24},{18,26},{20,28},{22,30},{32,40}... | collective-permute-start | bytes 884744 | tf_op jit(solution)/shard_map/ppermute | solution.py:409
  19.3 12.7 %collective-permute-start.1 = (bf16[4,144,256]{2,1,0:T(8,128)(2,1)S(1)}, bf16[4,144,256]{2,1,0:T(8,128)(2,1)S(1)}, u32[]{:S(2)}, u32[]{:S(2)}) collective-permute-start(bf16[4,144,256]{2,1,0:T(8,128)(2,1)S(1)} %slice.4), channel_id=1, source_target_pairs={{8,16},{10,18},{12,20},{14,22},{24,32},{26,34},{28,36},{30,38},{40... | collective-permute-start | bytes 884744 | tf_op jit(solution)/shard_map/ppermute | solution.py:410
  32.0 0.6 unpack.1
  32.6 5.0 %all-to-all-start.1 = ((f32[12,8,128]{2,1,0:T(8,128)}), f32[12,8,128]{2,1,0:T(8,128)S(1)}, u32[]{:S(2)}, u32[]{:S(2)}) async-start(f32[12,8,128]{2,1,0:T(8,128)} %unpack.1), calls=%async_computation.1 | async-start | bytes 98304 | tf_op jit(solution)/shard_map/all_to_all | solution.py:397
  37.6 0.1 pad_add_fusion.place_ref
  37.7 0.0 copy-done.2
  37.7 0.0 copy-done.1
  37.7 0.7 fetch.1
  38.4 9.5 %all-to-all-done.1.gathered_ref = f32[12,8,128]{2,1,0:T(8,128)S(1)} async-done(((f32[12,8,128]{2,1,0:T(8,128)}), f32[12,8,128]{2,1,0:T(8,128)S(1)}, u32[]{:S(2)}, u32[]{:S(2)}) %all-to-all-start.1) | async-done | bytes 49184 | tf_op jit(solution)/shard_map/all_to_all | solution.py:397
  47.9 0.5 interpolate.3
  48.4 2.6 %collective-permute-start.2 = (f32[16,256]{1,0:T(8,128)S(1)}, f32[16,256]{1,0:T(8,128)S(1)}, u32[]{:S(2)}, u32[]{:S(2)}) collective-permute-start(f32[16,256]{1,0:T(8,128)S(1)} %interpolate.3), channel_id=1, source_target_pairs={{0,96},{184,88},{2,98},{186,90},{4,100},{188,92},{6,102},{190,94},... | collective-permute-start | bytes 49160 | tf_op jit(solution)/shard_map/ppermute | solution.py:417
  51.0 0.1 add_convert_fusion.edge_ref
  51.1 1.3 %interpolate.2.fields_ref = f32[48,256]{1,0:T(8,128)S(1)} custom-call(f32[12,8,128]{2,1,0:T(8,128)S(1)} %all-to-all-done.1.gathered_ref, s32[4,4,1024]{2,1,0:T(4,128)S(1)} %get-tuple-element.7.code_ref, f32[4,4,1024]{2,1,0:T(4,128)S(1)} %get-tuple-element.8.share_ref, f32[4,4,256]{2,1,0:T(4,128)S(1)} %get-tuple-element.9.wet_ref), custom_call_target="tpu_custom_call" | custom-call | flops 6000000 | bytes 300000 | tf_op jit(solution)/shard_map/interpolate/pallas_call | solution.py:213
  52.4 2.9 %collective-permute-done.2.fother_ref = f32[16,256]{1,0:T(8,128)S(1)} collective-permute-done((f32[16,256]{1,0:T(8,128)S(1)}, f32[16,256]{1,0:T(8,128)S(1)}, u32[]{:S(2)}, u32[]{:S(2)}) %collective-permute-start.2) | collective-permute-done | bytes 16416 | tf_op jit(solution)/shard_map/ppermute | solution.py:417
  55.3 0.0 collective-permute-done.first_ref
  55.3 0.0 collective-permute-done.1.second_ref
  55.3 0.1 broadcast_in_dim.4.east_ref
  55.4 0.1 broadcast_in_dim.5.north_ref
  55.5 0.0 copy-start
  55.5 5.0 %propagate.1 = bf16[8,144,256]{2,1,0:T(8,128)(2,1)} custom-call(s32[3]{0:T(128)S(1)} %add_convert_fusion.edge_ref, bf16[4,144,256]{2,1,0:T(8,128)(2,1)S(1)} %collective-permute-done.first_ref, bf16[4,160,256]{2,1,0:T(8,128)(2,1)S(1)} %all-to-all-done.own_ref, bf16[4,144,256]{2,1,0:T(8,128)(2,1)S(1)} %collective-permute-done.1.second_ref, ...), custom_call_target="tpu_custom_call" | custom-call | flops 40000000 | bytes 1600000 | tf_op jit(solution)/shard_map/propagate/pallas_call | solution.py:299
  60.5 3.5 %all-to-all-start.2 = ((bf16[8,144,256]{2,1,0:T(8,128)(2,1)}), bf16[8,144,256]{2,1,0:T(8,128)(2,1)S(1)}, u32[]{:S(2)}, u32[]{:S(2)}) async-start(bf16[8,144,256]{2,1,0:T(8,128)(2,1)} %propagate.1), calls=%async_computation.2 | async-start | bytes 1179648 | tf_op jit(solution)/shard_map/all_to_all | solution.py:429
  64.0 0.1 multiply_convert_fusion.1
  64.2 10.6 %all-to-all-done.2 = bf16[8,144,256]{2,1,0:T(8,128)(2,1)S(1)} async-done(((bf16[8,144,256]{2,1,0:T(8,128)(2,1)}), bf16[8,144,256]{2,1,0:T(8,128)(2,1)S(1)}, u32[]{:S(2)}, u32[]{:S(2)}) %all-to-all-start.2) | async-done | bytes 589856 | tf_op jit(solution)/shard_map/all_to_all | solution.py:429
  74.7 0.0 copy-done
  74.7 1.4 %finish.1 = (bf16[576,256]{1,0:T(8,128)(2,1)}, f32[32,256]{1,0:T(8,128)}) custom-call(s32[1]{0:T(128)} %bitcast.comp_ref, bf16[1152,256]{1,0:T(8,128)(2,1)S(1)} %bitcast.13, bf16[576,1152]{1,0:T(8,128)(2,1)S(1)} %copy-done, bf16[32,1152]{1,0:T(8,128)(2,1)S(1)} %pad_maximum_fusion.kernel_ref, f32[1,256]{1,0:T(1,128)S(1)} %dynamic-slice_convert_fusion.wet_ref), custom_call_target="tpu_custom_call" | custom-call | flops 358612992 | bytes 2500000 | tf_op jit(solution)/shard_map/finish/pallas_call | solution.py:348
  (5 shorter events, 0.1 us)
Async XLA Ops:
  0.6 6.2 %copy-start.3 = (s32[48,256]{1,0:T(8,128)S(1)}, s32[48,256]{1,0:T(8,128)}, u32[]{:S(2)}) copy-start(s32[48,256]{1,0:T(8,128)} %mask_ref.1) | copy-start | bytes 147460
  0.6 37.0 %copy-start.2 = (f32[4,12288]{1,0:T(4,128)S(1)}, f32[4,12288]{1,0:T(4,128)}, u32[]{:S(2)}) copy-start(f32[4,12288]{1,0:T(4,128)} %weight_ref.1) | copy-start | bytes 589828
  0.7 37.0 %copy-start.1 = (s32[4,12288]{1,0:T(4,128)S(1)}, s32[4,12288]{1,0:T(4,128)}, u32[]{:S(2)}) copy-start(s32[4,12288]{1,0:T(4,128)} %index_ref.1) | copy-start | bytes 589828
  2.5 12.5 %all-to-all-start = ((bf16[4,160,256]{2,1,0:T(8,128)(2,1)}), bf16[4,160,256]{2,1,0:T(8,128)(2,1)S(1)}, u32[]{:S(2)}, u32[]{:S(2)}) async-start(bf16[4,160,256]{2,1,0:T(8,128)(2,1)} %pack.1), calls=%async_computation | async-start | bytes 655360 | tf_op jit(solution)/shard_map/all_to_all | solution.py:384
  15.0 40.3 %collective-permute-start = (bf16[4,144,256]{2,1,0:T(8,128)(2,1)S(1)}, bf16[4,144,256]{2,1,0:T(8,128)(2,1)S(1)}, u32[]{:S(2)}, u32[]{:S(2)}) collective-permute-start(bf16[4,144,256]{2,1,0:T(8,128)(2,1)S(1)} %slice.4), channel_id=1, source_target_pairs={{0,8},{2,10},{4,12},{6,14},{16,24},{18,26},{20,28},{22,30},{32,40}... | collective-permute-start | bytes 884744 | tf_op jit(solution)/shard_map/ppermute | solution.py:409
  19.3 36.0 %collective-permute-start.1 = (bf16[4,144,256]{2,1,0:T(8,128)(2,1)S(1)}, bf16[4,144,256]{2,1,0:T(8,128)(2,1)S(1)}, u32[]{:S(2)}, u32[]{:S(2)}) collective-permute-start(bf16[4,144,256]{2,1,0:T(8,128)(2,1)S(1)} %slice.4), channel_id=1, source_target_pairs={{8,16},{10,18},{12,20},{14,22},{24,32},{26,34},{28,36},{30,38},{40... | collective-permute-start | bytes 884744 | tf_op jit(solution)/shard_map/ppermute | solution.py:410
  32.6 15.4 %all-to-all-start.1 = ((f32[12,8,128]{2,1,0:T(8,128)}), f32[12,8,128]{2,1,0:T(8,128)S(1)}, u32[]{:S(2)}, u32[]{:S(2)}) async-start(f32[12,8,128]{2,1,0:T(8,128)} %unpack.1), calls=%async_computation.1 | async-start | bytes 98304 | tf_op jit(solution)/shard_map/all_to_all | solution.py:397
  48.4 6.8 %collective-permute-start.2 = (f32[16,256]{1,0:T(8,128)S(1)}, f32[16,256]{1,0:T(8,128)S(1)}, u32[]{:S(2)}, u32[]{:S(2)}) collective-permute-start(f32[16,256]{1,0:T(8,128)S(1)} %interpolate.3), channel_id=1, source_target_pairs={{0,96},{184,88},{2,98},{186,90},{4,100},{188,92},{6,102},{190,94},... | collective-permute-start | bytes 49160 | tf_op jit(solution)/shard_map/ppermute | solution.py:417
  55.5 19.3 %copy-start = (bf16[576,1152]{1,0:T(8,128)(2,1)S(1)}, bf16[576,1152]{1,0:T(8,128)(2,1)}, u32[]{:S(2)}) copy-start(bf16[576,1152]{1,0:T(8,128)(2,1)} %source_ref.1) | copy-start | bytes 3981316
  60.5 14.2 %all-to-all-start.2 = ((bf16[8,144,256]{2,1,0:T(8,128)(2,1)}), bf16[8,144,256]{2,1,0:T(8,128)(2,1)S(1)}, u32[]{:S(2)}, u32[]{:S(2)}) async-start(bf16[8,144,256]{2,1,0:T(8,128)(2,1)} %propagate.1), calls=%async_computation.2 | async-start | bytes 1179648 | tf_op jit(solution)/shard_map/all_to_all | solution.py:429
